TPU v7x, 32 devices: a whole 2x2x4 slice. The times are simulated.
32 devices in a mesh: row: 16 (over z, y, x), col: 2 (over core).
Axes of the slice: x: 2, y: 2, z: 4, core: 2. Of those that a mesh axis runs over, the one named last changes fastest.
Arguments:
- offsets: float32 [2, 32768], P(None, ('row', 'col')), may hold values from 0 to 1
- site_cell: int32 [32768], P(('row', 'col')), may hold values from 0 to 511, as said below
- estimates: float32 [4, 64, 8], P(None, 'row', 'col'), may hold values from -0.7 to 0.7
- panel_tile: int32 [1], replicated, may hold values from 0 to 63
Outputs:
- panel: float32 [512, 32768], P('col', 'row')
- fields: float32 [4, 32768], P(None, ('row', 'col'))
Inputs may be any that keep to these rules, and one draw needn't show every extreme that they name: `site_cell`: the site with global index g lies on device number g // 1024 of the row-major (row) by (col) grid of devices; for device (r, c) its cell's first index lies in r * 4 to r * 4 + 3 and its second index in c * 4 to c * 4 + 3.
All inputs are finite; a program needn't handle non-finite values.
Results may differ from a plain program's by a relative error of at most 0.0003.
Values sent between devices are 32-bit elements; how exact they have to be, the bound alone decides.
No kernel may reach another device: no remote copies, remote signals or barrier semaphores. Data moves between devices by JAX's collectives and lax.ppermute only.
A program may use at most 64 MiB of HBM per device.

v0:
```python
import functools

import jax
import jax.numpy as jnp
from jax import lax
from jax.experimental import pallas as pl
from jax.experimental.pallas import tpu as pltpu
from jax.sharding import PartitionSpec as P

SITE_DEV = 1024
TILE = 512
CELL_X = 4
CELL_Y = 4
RADIUS = 2

spread_cells = 1.5
nugget_share = 0.5
range_shift = -0.7

LANES = 128
BLOCK = 128
FIELDS = 4
SITE_ROWS = SITE_DEV // LANES
TILE_ROWS = TILE // LANES
HEAD = 3 * TILE_ROWS
CHUNK = 256
QUANT = 6

HIGHEST = lax.Precision.HIGHEST


def dot(a, b):
    return jnp.dot(a, b, precision=HIGHEST, preferred_element_type=jnp.float32)


def dot_t(a, b):
    return lax.dot_general(
        a, b, (((1,), (1,)), ((), ())), precision=HIGHEST, preferred_element_type=jnp.float32
    )


def pack_kernel(cols, tile_ref, est_ref, offsets_ref, cell_ref, raw_ref, buf_ref):
    row = lax.axis_index("row")
    col = lax.axis_index("col")
    for j in range(SITE_ROWS):
        part = slice(j * LANES, (j + 1) * LANES)
        raw_ref[j : j + 1, :] = offsets_ref[0:1, part]
        raw_ref[SITE_ROWS + j : SITE_ROWS + j + 1, :] = offsets_ref[1:2, part]
        raw_ref[2 * SITE_ROWS + j : 2 * SITE_ROWS + j + 1, :] = cell_ref[0:1, part].astype(
            jnp.float32
        )
    start = tile_ref[0] * TILE
    root = start // SITE_DEV
    first = (start - root * SITE_DEV) // LANES
    mine = row * cols + col == root
    for q in range(3):
        rows = raw_ref[pl.ds(q * SITE_ROWS + first, TILE_ROWS), :]
        buf_ref[q * TILE_ROWS : (q + 1) * TILE_ROWS, :] = jnp.where(mine, rows, 0.0)
    grid_y = cols * CELL_Y
    lane = lax.broadcasted_iota(jnp.int32, (1, LANES), 1) - col * CELL_Y
    line = jnp.zeros((1, LANES), jnp.float32)
    for f in range(FIELDS):
        for a in range(CELL_X):
            for b in range(CELL_Y):
                line = jnp.where(
                    lane == (f * CELL_X + a) * grid_y + b, est_ref[f, a, b], line
                )
    count = buf_ref.shape[0] - HEAD
    index = lax.broadcasted_iota(jnp.int32, (count, LANES), 0)
    buf_ref[HEAD:, :] = jnp.where(index == row, jnp.broadcast_to(line, (count, LANES)), 0.0)


def smooth(raw, block_row, table_ref, rows_mesh, grid_y):
    off_x, off_y, cell = raw
    total_x = CELL_X * rows_mesh
    cell_x = jnp.floor((cell + 0.5) / grid_y)
    cell_y = cell - cell_x * grid_y
    loc_x = cell_x + off_x
    loc_y = cell_y + off_y
    weight_y = []
    for b in range(grid_y):
        dist = loc_y - (b + 0.5)
        value = jnp.exp(-dist * dist / (2.0 * spread_cells * spread_cells))
        weight_y.append(jnp.where(jnp.abs(cell_y - b) <= RADIUS, value, 0.0))
    sum_y = functools.reduce(jnp.add, weight_y)
    numer = [None] * FIELDS
    sum_x = None
    for a in range(CELL_X - RADIUS, 2 * CELL_X + RADIUS):
        coord = (block_row - 1) * CELL_X + a
        near = block_row - 1 + a // CELL_X
        line = HEAD + jnp.clip(near, 0, rows_mesh - 1)
        coord_f = coord.astype(jnp.float32)
        dist = loc_x - coord_f - 0.5
        value = jnp.exp(-dist * dist / (2.0 * spread_cells * spread_cells))
        inside = (coord >= 0) & (coord < total_x)
        reach = jnp.where(inside, float(RADIUS), -1.0)
        weight = jnp.where(jnp.abs(cell_x - coord_f) <= reach, value, 0.0)
        sum_x = weight if sum_x is None else sum_x + weight
        for f in range(FIELDS):
            base = (f * CELL_X + a % CELL_X) * grid_y
            inner = None
            for b in range(grid_y):
                term = table_ref[line, base + b] * weight_y[b]
                inner = term if inner is None else inner + term
            term = inner * weight
            numer[f] = term if numer[f] is None else numer[f] + term
    denom = sum_x * sum_y
    return [n / denom for n in numer], loc_x, loc_y


def quantities(fields, loc_x, loc_y, total_x):
    first = jnp.exp(2.0 * (fields[0] + range_shift))
    second = jnp.exp(2.0 * (fields[1] + range_shift))
    cosine = jnp.cos(fields[2])
    sine = jnp.sin(fields[2])
    half_a = 0.5 * (cosine * cosine * first + sine * sine * second)
    half_b = 0.5 * (sine * sine * first + cosine * cosine * second)
    half_c = 0.5 * (cosine * sine * (first - second))
    scale = jnp.exp(fields[3] + 0.5 * (fields[0] + fields[1] + 2.0 * range_shift))
    return [half_a, half_b, half_c, loc_x / total_x, loc_y / total_x, scale]


def covariance(cols, rows):
    m_aa = cols[0] + rows[0]
    m_bb = cols[1] + rows[1]
    m_ab = cols[2] + rows[2]
    diff_x = cols[3] - rows[3]
    diff_y = cols[4] - rows[4]
    inv_root = lax.rsqrt(m_aa * m_bb - m_ab * m_ab)
    form = diff_x * (m_bb * diff_x - m_ab * diff_y) + diff_y * (m_aa * diff_y - m_ab * diff_x)
    square = jnp.maximum(form * (3.0 * inv_root * inv_root), 1e-36)
    dist = square * lax.rsqrt(square)
    return (cols[5] * rows[5]) * inv_root * (1.0 + dist) * jnp.exp(-dist)


def lane_copy(values, lane):
    index = jnp.full(values.shape, lane, jnp.int32)
    return jnp.take_along_axis(values, index, axis=1)


def row_copy(values, row):
    return jnp.broadcast_to(values[row : row + 1, :], values.shape)


def inverse_factor(rows):
    steps = BLOCK // 8
    lane = lax.broadcasted_iota(jnp.int32, (8, BLOCK), 1)
    sub = lax.broadcasted_iota(jnp.int32, (8, BLOCK), 0)
    rows = list(rows)
    out = [None] * steps
    for m in range(steps):
        at = 8 * m
        pivots = (lane >= at) & (lane < at + 8)
        column = [lane_copy(rows[m], at + c) for c in range(8)]
        block = jnp.where(lane - at == sub, 1.0, jnp.where(pivots, 0.0, rows[m]))
        solved = None
        inverse = None
        for c in range(8):
            pivot = row_copy(column[c], c)
            inv = 1.0 / pivot
            line = row_copy(block, c)
            scaled = line * lax.rsqrt(pivot)
            solved = scaled if c == 0 else jnp.where(sub == c, scaled, solved)
            inverse = inv if c == 0 else jnp.where(sub == c, inv, inverse)
            others = jnp.where(sub == c, 0.0, column[c])
            for j in range(c + 1, 8):
                column[j] = column[j] - (others * row_copy(column[j], c)) * inv
            block = block - (others * line) * inv
        out[m] = solved
        if m == steps - 1:
            break
        block = block * inverse
        lines = [row_copy(block, c) for c in range(8)]
        for i in range(m + 1, steps):
            p = [lane_copy(rows[i], at + c) * lines[c] for c in range(8)]
            total = ((p[0] + p[1]) + (p[2] + p[3])) + ((p[4] + p[5]) + (p[6] + p[7]))
            rows[i] = jnp.where(pivots, 0.0, rows[i]) - total
    result = jnp.concatenate(out, axis=0)
    r = lax.broadcasted_iota(jnp.int32, (BLOCK, BLOCK), 0)
    c = lax.broadcasted_iota(jnp.int32, (BLOCK, BLOCK), 1)
    return jnp.where(c <= r, result, 0.0)


def at(block):
    return slice(block * BLOCK, (block + 1) * BLOCK)


def main_kernel(
    rows_mesh, cols, tile_ref, table_ref, buf_ref, *refs
):
    raws = refs[:cols]
    panel_ref, fields_ref, colq, rowq, siteq, gram, inv, solved, cov, sems = refs[cols:]
    row = lax.axis_index("row")
    col = lax.axis_index("col")
    grid_y = cols * CELL_Y
    total_x = float(CELL_X * rows_mesh)
    width = TILE // cols
    start = tile_ref[0] * TILE
    root_row = start // (SITE_DEV * cols)
    blocks = TILE // BLOCK
    lane = lax.broadcasted_iota(jnp.int32, (8, BLOCK), 1)
    sub = lax.broadcasted_iota(jnp.int32, (8, BLOCK), 0)

    raw = [buf_ref[q * TILE_ROWS : (q + 1) * TILE_ROWS, :] for q in range(3)]
    fields, loc_x, loc_y = smooth(raw, root_row, table_ref, rows_mesh, grid_y)
    quant = quantities(fields, loc_x, loc_y, total_x)
    nugget = nugget_share * jnp.exp(2.0 * fields[3])
    for q in range(QUANT):
        rowq[q, :, :] = quant[q]
    rowq[QUANT, :, :] = nugget
    for g in range(TILE_ROWS):
        stack = jnp.concatenate(
            [quant[q][g : g + 1, :] for q in range(QUANT)] + [jnp.zeros((2, LANES), jnp.float32)],
            axis=0,
        )
        turned = jnp.transpose(stack)
        for q in range(QUANT):
            colq[q, g * LANES : (g + 1) * LANES, :] = jnp.broadcast_to(
                turned[:, q : q + 1], (LANES, LANES)
            )

    for k in range(cols):
        member = jnp.bitwise_xor(col, k)
        raw = [raws[k][q * SITE_ROWS : (q + 1) * SITE_ROWS, :] for q in range(3)]
        fields, loc_x, loc_y = smooth(raw, row, table_ref, rows_mesh, grid_y)
        if k == 0:
            for f in range(FIELDS):
                for j in range(SITE_ROWS):
                    fields_ref[f : f + 1, j * LANES : (j + 1) * LANES] = fields[f][j : j + 1, :]
        quant = quantities(fields, loc_x, loc_y, total_x)
        for q in range(QUANT):
            siteq[q, pl.ds(pl.multiple_of(member * SITE_ROWS, 8), SITE_ROWS), :] = quant[q]

    for j in range(blocks):
        lines = [jnp.broadcast_to(rowq[q, j : j + 1, :], (16, LANES)) for q in range(QUANT)]

        def tile_step(t, carry, j=j, lines=lines):
            base = pl.multiple_of(t * 16, 16)
            pick = [colq[q, pl.ds(base, 16), :] for q in range(QUANT)]
            gram[pl.ds(base, 16), at(j)] = covariance(pick, lines)
            return carry

        lax.fori_loop(j * BLOCK // 16, TILE // 16, tile_step, 0)

    for k in range(blocks):
        diagonal = []
        for i in range(BLOCK // 8):
            values = gram[k * BLOCK + 8 * i : k * BLOCK + 8 * i + 8, at(k)]
            nug = jnp.broadcast_to(rowq[QUANT, k : k + 1, :], (8, BLOCK))
            diagonal.append(values + jnp.where(lane - 8 * i == sub, nug, 0.0))
        own = inverse_factor(diagonal)
        inv[at(k), at(k)] = own
        if k > 0:
            inv[at(k), : k * BLOCK] = dot(own, inv[at(k), : k * BLOCK])
        if k + 1 < blocks:
            rest = slice((k + 1) * BLOCK, TILE)
            lower = dot_t(gram[rest, at(k)], own)
            for i in range(k + 1, blocks):
                mine = lower[(i - k - 1) * BLOCK : (i - k) * BLOCK, :]
                upto = slice((k + 1) * BLOCK, (i + 1) * BLOCK)
                gram[at(i), upto] = gram[at(i), upto] - dot_t(mine, lower[: (i - k) * BLOCK, :])
            if k > 0:
                inv[rest, : k * BLOCK] = inv[rest, : k * BLOCK] - dot(
                    lower, inv[at(k), : k * BLOCK]
                )
            inv[rest, at(k)] = -dot(lower, own)

    first = pl.multiple_of(col * width, width)
    depth = (col + 1) * (width // BLOCK)
    chunks = cols * SITE_DEV // CHUNK
    parts = CHUNK // LANES
    eye = lax.broadcasted_iota(jnp.int32, (BLOCK, LANES), 0) == lax.broadcasted_iota(
        jnp.int32, (BLOCK, LANES), 1
    )

    def chunk_step(ch, carry):
        lines = [
            [
                jnp.broadcast_to(siteq[q, pl.ds(ch * parts + p, 1), :], (8, LANES))
                for q in range(QUANT)
            ]
            for p in range(parts)
        ]
        here = pl.multiple_of(ch * CHUNK, CHUNK)

        def depth_step(kb, carry):
            base = pl.multiple_of(kb * BLOCK, BLOCK)
            for t in range(BLOCK // 8):
                pick = [colq[q, pl.ds(base + 8 * t, 8), :] for q in range(QUANT)]
                for p in range(parts):
                    cov[8 * t : 8 * t + 8, p * LANES : (p + 1) * LANES] = covariance(
                        pick, lines[p]
                    )
            for p in range(parts):
                same = start + base == row * (cols * SITE_DEV) + here + p * LANES

                @pl.when(same)
                def _(p=p):
                    nug = jnp.broadcast_to(rowq[QUANT, pl.ds(kb, 1), :], (BLOCK, LANES))
                    part = slice(p * LANES, (p + 1) * LANES)
                    cov[:, part] = cov[:, part] + jnp.where(eye, nug, 0.0)

            product = dot(inv[pl.ds(first, width), pl.ds(base, BLOCK)], cov[...])

            @pl.when(kb == 0)
            def _():
                solved[:, pl.ds(here, CHUNK)] = product

            @pl.when(kb > 0)
            def _():
                solved[:, pl.ds(here, CHUNK)] = solved[:, pl.ds(here, CHUNK)] + product

            return carry

        lax.fori_loop(0, depth, depth_step, 0)
        pltpu.make_async_copy(
            solved.at[:, pl.ds(here, CHUNK)], panel_ref.at[:, pl.ds(here, CHUNK)], sems.at[ch]
        ).start()
        return carry

    lax.fori_loop(0, chunks, chunk_step, 0)

    def finish(ch, carry):
        here = pl.multiple_of(ch * CHUNK, CHUNK)
        pltpu.make_async_copy(
            solved.at[:, pl.ds(here, CHUNK)], panel_ref.at[:, pl.ds(here, CHUNK)], sems.at[ch]
        ).wait()
        return carry

    lax.fori_loop(0, chunks, finish, 0)


def body(offsets, site_cell, estimates, panel_tile):
    rows_mesh = lax.axis_size("row")
    cols = lax.axis_size("col")
    devices = rows_mesh * cols
    assert FIELDS * CELL_X * CELL_Y * cols == LANES
    assert devices & (devices - 1) == 0
    vmem = pl.BlockSpec(memory_space=pltpu.VMEM)
    smem = pl.BlockSpec(memory_space=pltpu.SMEM)
    raw, buf = pl.pallas_call(
        functools.partial(pack_kernel, cols),
        out_shape=(
            jax.ShapeDtypeStruct((3 * SITE_ROWS, LANES), jnp.float32),
            jax.ShapeDtypeStruct((HEAD + rows_mesh, LANES), jnp.float32),
        ),
        in_specs=[smem, smem, vmem, vmem],
        out_specs=(vmem, vmem),
    )(panel_tile, estimates, offsets, site_cell.reshape(1, -1))
    raws = [raw]
    for k in range(1, cols):
        raws.append(lax.ppermute(raw, "col", [(i, i ^ k) for i in range(cols)]))
    step = 1
    while step < devices:
        pairs = [(i, i ^ step) for i in range(devices)]
        buf = buf + lax.ppermute(buf, ("row", "col"), pairs)
        step *= 2
    width = TILE // cols
    sites = cols * SITE_DEV
    panel, fields = pl.pallas_call(
        functools.partial(main_kernel, rows_mesh, cols),
        out_shape=(
            jax.ShapeDtypeStruct((width, sites), jnp.float32),
            jax.ShapeDtypeStruct((FIELDS, SITE_DEV), jnp.float32),
        ),
        in_specs=[smem, smem, vmem] + [vmem] * cols,
        out_specs=(pl.BlockSpec(memory_space=pl.ANY), vmem),
        scratch_shapes=[
            pltpu.VMEM((QUANT, TILE, LANES), jnp.float32),
            pltpu.VMEM((QUANT + 1, TILE_ROWS, LANES), jnp.float32),
            pltpu.VMEM((QUANT, cols * SITE_ROWS, LANES), jnp.float32),
            pltpu.VMEM((TILE, TILE), jnp.float32),
            pltpu.VMEM((TILE, TILE), jnp.float32),
            pltpu.VMEM((width, sites), jnp.float32),
            pltpu.VMEM((BLOCK, CHUNK), jnp.float32),
            pltpu.SemaphoreType.DMA((sites // CHUNK,)),
        ],
        compiler_params=pltpu.CompilerParams(vmem_limit_bytes=40 * 1024 * 1024),
    )(panel_tile, buf, buf, *raws)
    return (panel, fields)


def solution(mesh):
    placed = (P(None, ("row", "col")), P(("row", "col")), P(None, "row", "col"), P())
    return jax.shard_map(
        body,
        mesh=mesh,
        in_specs=placed,
        out_specs=(P("col", "row"), P(None, ("row", "col"))),
        check_vma=False,
    )
```

profile of v0, /device:TPU:1, one launch (start us, length us, event | category | flops | bytes accessed | tf_op | source)
XLA Modules:
  0.0 61.2 jit_solution(5676867276522027444)
XLA Ops:
  1.3 1.5 %shard_map.59 = (f32[24,128]{1,0:T(8,128)}, f32[28,128]{1,0:T(8,128)}) custom-call(s32[1]{0:T(128)S(6)} %copy.6.tile_ref, f32[4,4,4]{2,1,0:T(4,128)} %est_ref.1, f32[2,1024]{1,0:T(2,128)} %offsets_ref.1, s32[1,1024]{1,0:T(1,128)} %bitcast.1), custom_call_target="tpu_custom_call" | custom-call | tf_op jit(solution)/shard_map/pallas_call | solution.py:341
  2.7 0.0 collective-permute-start
  2.8 1.4 %collective-permute-done = f32[28,128]{1,0:T(8,128)S(1)} collective-permute-done((f32[28,128]{1,0:T(8,128)}, f32[28,128]{1,0:T(8,128)S(1)}, u32[]{:S(2)}, u32[]{:S(2)}) %collective-permute-start) | collective-permute-done | bytes 14368 | tf_op jit(solution)/shard_map/ppermute | solution.py:356
  4.1 0.7 %add.15 = f32[28,128]{1,0:T(8,128)S(1)} add(f32[28,128]{1,0:T(8,128)} %get-tuple-element.4, f32[28,128]{1,0:T(8,128)S(1)} %collective-permute-done) | non-fusion elementwise | flops 3584 | bytes 43008 | tf_op jit(solution)/shard_map/add | solution.py:356
  4.9 2.4 %collective-permute-start.1 = (f32[28,128]{1,0:T(8,128)S(1)}, f32[28,128]{1,0:T(8,128)S(1)}, u32[]{:S(2)}, u32[]{:S(2)}) collective-permute-start(f32[28,128]{1,0:T(8,128)S(1)} %add.15), channel_id=1, source_target_pairs={{0,2},{1,3},{2,0},{3,1},{4,6},{5,7},{6,4},{7,5},{8,10},{9,11},{10,... | collective-permute-start | bytes 43016 | tf_op jit(solution)/shard_map/ppermute | solution.py:356
  7.2 1.1 %collective-permute-done.1 = f32[28,128]{1,0:T(8,128)S(1)} collective-permute-done((f32[28,128]{1,0:T(8,128)S(1)}, f32[28,128]{1,0:T(8,128)S(1)}, u32[]{:S(2)}, u32[]{:S(2)}) %collective-permute-start.1) | collective-permute-done | bytes 14368 | tf_op jit(solution)/shard_map/ppermute | solution.py:356
  8.3 1.5 %collective-permute-start.2 = (f32[28,128]{1,0:T(8,128)S(1)}, f32[28,128]{1,0:T(8,128)S(1)}, u32[]{:S(2)}, u32[]{:S(2)}) collective-permute-start(f32[28,128]{1,0:T(8,128)S(1)} %add.16), channel_id=1, source_target_pairs={{0,4},{1,5},{2,6},{3,7},{4,0},{5,1},{6,2},{7,3},{8,12},{9,13},{10,... | collective-permute-start | bytes 43016 | tf_op jit(solution)/shard_map/ppermute | solution.py:356
  9.8 1.1 %collective-permute-done.2 = f32[28,128]{1,0:T(8,128)S(1)} collective-permute-done((f32[28,128]{1,0:T(8,128)S(1)}, f32[28,128]{1,0:T(8,128)S(1)}, u32[]{:S(2)}, u32[]{:S(2)}) %collective-permute-start.2) | collective-permute-done | bytes 14368 | tf_op jit(solution)/shard_map/ppermute | solution.py:356
  11.0 1.5 %collective-permute-start.3 = (f32[28,128]{1,0:T(8,128)S(1)}, f32[28,128]{1,0:T(8,128)S(1)}, u32[]{:S(2)}, u32[]{:S(2)}) collective-permute-start(f32[28,128]{1,0:T(8,128)S(1)} %add.17), channel_id=1, source_target_pairs={{0,8},{1,9},{2,10},{3,11},{4,12},{5,13},{6,14},{7,15},{8,0},{9,1},... | collective-permute-start | bytes 43016 | tf_op jit(solution)/shard_map/ppermute | solution.py:356
  12.5 1.1 %collective-permute-done.3 = f32[28,128]{1,0:T(8,128)S(1)} collective-permute-done((f32[28,128]{1,0:T(8,128)S(1)}, f32[28,128]{1,0:T(8,128)S(1)}, u32[]{:S(2)}, u32[]{:S(2)}) %collective-permute-start.3) | collective-permute-done | bytes 14368 | tf_op jit(solution)/shard_map/ppermute | solution.py:356
  13.6 2.5 %collective-permute-start.4 = (f32[28,128]{1,0:T(8,128)S(1)}, f32[28,128]{1,0:T(8,128)S(1)}, u32[]{:S(2)}, u32[]{:S(2)}) collective-permute-start(f32[28,128]{1,0:T(8,128)S(1)} %add.18), channel_id=1, source_target_pairs={{0,16},{1,17},{2,18},{3,19},{4,20},{5,21},{6,22},{7,23},{8,24},{9,... | collective-permute-start | bytes 43016 | tf_op jit(solution)/shard_map/ppermute | solution.py:356
  16.1 4.1 %collective-permute-start.5 = (f32[24,128]{1,0:T(8,128)}, f32[24,128]{1,0:T(8,128)S(1)}, u32[]{:S(2)}, u32[]{:S(2)}) collective-permute-start(f32[24,128]{1,0:T(8,128)} %get-tuple-element.5.refs_0_), channel_id=1, source_target_pairs={{0,1},{1,0},{2,3},{3,2},{4,5},{5,4},{6,7},{7,6},{8,9},{9,8},{10,11... | collective-permute-start | bytes 36872 | tf_op jit(solution)/shard_map/ppermute | solution.py:352
  20.2 0.0 collective-permute-done.4
  20.2 1.0 %collective-permute-done.5.refs_1_ = f32[24,128]{1,0:T(8,128)S(1)} collective-permute-done((f32[24,128]{1,0:T(8,128)}, f32[24,128]{1,0:T(8,128)S(1)}, u32[]{:S(2)}, u32[]{:S(2)}) %collective-permute-start.5) | collective-permute-done | bytes 12320 | tf_op jit(solution)/shard_map/ppermute | solution.py:352
  21.2 0.0 copy-start
  21.2 0.7 %copy-done = f32[24,128]{1,0:T(8,128)S(1)} copy-done((f32[24,128]{1,0:T(8,128)S(1)}, f32[24,128]{1,0:T(8,128)}, u32[]{:S(2)}) %copy-start) | copy-done | bytes 12312
  21.9 39.3 %shard_map.60 = (f32[256,2048]{1,0:T(8,128)}, f32[4,1024]{1,0:T(4,128)}) custom-call(s32[1]{0:T(128)S(6)} %copy.6.tile_ref, f32[28,128]{1,0:T(8,128)S(1)} %add.19.table_ref.buf_ref, f32[28,128]{1,0:T(8,128)S(1)} %add.19.table_ref.buf_ref, f32[24,128]{1,0:T(8,128)S(1)} %copy-done, f32[24,128]{1,0:T(8,128)S(1)} %collective-permute-done.5.refs_1_), custom_call_target="tpu_custom_call" | custom-call | tf_op jit(solution)/shard_map/pallas_call | solution.py:360
  (4 shorter events, 0.0 us)
Async XLA Ops:
  2.7 1.4 %collective-permute-start = (f32[28,128]{1,0:T(8,128)}, f32[28,128]{1,0:T(8,128)S(1)}, u32[]{:S(2)}, u32[]{:S(2)}) collective-permute-start(f32[28,128]{1,0:T(8,128)} %get-tuple-element.4), channel_id=1, source_target_pairs={{0,1},{1,0},{2,3},{3,2},{4,5},{5,4},{6,7},{7,6},{8,9},{9,8},{10,11... | collective-permute-start | bytes 43016 | tf_op jit(solution)/shard_map/ppermute | solution.py:356
  4.9 3.5 %collective-permute-start.1 = (f32[28,128]{1,0:T(8,128)S(1)}, f32[28,128]{1,0:T(8,128)S(1)}, u32[]{:S(2)}, u32[]{:S(2)}) collective-permute-start(f32[28,128]{1,0:T(8,128)S(1)} %add.15), channel_id=1, source_target_pairs={{0,2},{1,3},{2,0},{3,1},{4,6},{5,7},{6,4},{7,5},{8,10},{9,11},{10,... | collective-permute-start | bytes 43016 | tf_op jit(solution)/shard_map/ppermute | solution.py:356
  8.3 2.6 %collective-permute-start.2 = (f32[28,128]{1,0:T(8,128)S(1)}, f32[28,128]{1,0:T(8,128)S(1)}, u32[]{:S(2)}, u32[]{:S(2)}) collective-permute-start(f32[28,128]{1,0:T(8,128)S(1)} %add.16), channel_id=1, source_target_pairs={{0,4},{1,5},{2,6},{3,7},{4,0},{5,1},{6,2},{7,3},{8,12},{9,13},{10,... | collective-permute-start | bytes 43016 | tf_op jit(solution)/shard_map/ppermute | solution.py:356
  11.0 2.6 %collective-permute-start.3 = (f32[28,128]{1,0:T(8,128)S(1)}, f32[28,128]{1,0:T(8,128)S(1)}, u32[]{:S(2)}, u32[]{:S(2)}) collective-permute-start(f32[28,128]{1,0:T(8,128)S(1)} %add.17), channel_id=1, source_target_pairs={{0,8},{1,9},{2,10},{3,11},{4,12},{5,13},{6,14},{7,15},{8,0},{9,1},... | collective-permute-start | bytes 43016 | tf_op jit(solution)/shard_map/ppermute | solution.py:356
  13.6 6.6 %collective-permute-start.4 = (f32[28,128]{1,0:T(8,128)S(1)}, f32[28,128]{1,0:T(8,128)S(1)}, u32[]{:S(2)}, u32[]{:S(2)}) collective-permute-start(f32[28,128]{1,0:T(8,128)S(1)} %add.18), channel_id=1, source_target_pairs={{0,16},{1,17},{2,18},{3,19},{4,20},{5,21},{6,22},{7,23},{8,24},{9,... | collective-permute-start | bytes 43016 | tf_op jit(solution)/shard_map/ppermute | solution.py:356
  16.1 5.1 %collective-permute-start.5 = (f32[24,128]{1,0:T(8,128)}, f32[24,128]{1,0:T(8,128)S(1)}, u32[]{:S(2)}, u32[]{:S(2)}) collective-permute-start(f32[24,128]{1,0:T(8,128)} %get-tuple-element.5.refs_0_), channel_id=1, source_target_pairs={{0,1},{1,0},{2,3},{3,2},{4,5},{5,4},{6,7},{7,6},{8,9},{9,8},{10,11... | collective-permute-start | bytes 36872 | tf_op jit(solution)/shard_map/ppermute | solution.py:352
  21.2 0.7 %copy-start = (f32[24,128]{1,0:T(8,128)S(1)}, f32[24,128]{1,0:T(8,128)}, u32[]{:S(2)}) copy-start(f32[24,128]{1,0:T(8,128)} %get-tuple-element.5.refs_0_) | copy-start | bytes 36868
where the time goes:
time: 61.6 us; the launch traced here: 61.2 us
  Pallas kernels  40.8 us (66%)
  starting transfers between devices  11.9 us (19%)
  waiting for transfers between devices  5.79 us (9%)
  between operations  1.29 us (2%)
  other arithmetic  0.74 us (1%)
  local copies, waits for them, and re-layouts  0.71 us (1%)
    pallas_call x1, Pallas kernels, body(): pl.pallas_call(functools.partial(main_kernel, rows_mesh, cols), out_shape...  39.3 us
    ppermute x5, starting transfers between devices, body(): buf = buf + lax.ppermute(buf, ('row', 'col'), pairs)  7.86 us
    ppermute x5, waiting for transfers between devices, body(): buf = buf + lax.ppermute(buf, ('row', 'col'), pairs)  4.76 us
    ppermute x1, starting transfers between devices, body(): raws.append(lax.ppermute(raw, 'col', [(i, i ^ k) for i in range(cols)]))  4.07 us
    pallas_call x1, Pallas kernels, body(): pl.pallas_call(functools.partial(pack_kernel, cols), out_shape=(jax.Shape...  1.46 us
  transfers between devices with their start and end apart: 6, of which 5 were waited for; matrix products, arithmetic and copies ran while one was open for 0% of the time, Pallas kernels for 0%

commit v1 on v0

--- a/solution.py
+++ b/solution.py
@@ -142,7 +142,7 @@
     return jnp.broadcast_to(values[row : row + 1, :], values.shape)
 
 
-def inverse_factor(rows):
+def inverse_factor(rows, beside):
     steps = BLOCK // 8
     lane = lax.broadcasted_iota(jnp.int32, (8, BLOCK), 1)
     sub = lax.broadcasted_iota(jnp.int32, (8, BLOCK), 0)
@@ -167,6 +167,7 @@
                 column[j] = column[j] - (others * row_copy(column[j], c)) * inv
             block = block - (others * line) * inv
         out[m] = solved
+        beside(m)
         if m == steps - 1:
             break
         block = block * inverse
@@ -185,11 +186,9 @@
     return slice(block * BLOCK, (block + 1) * BLOCK)
 
 
-def main_kernel(
-    rows_mesh, cols, tile_ref, table_ref, buf_ref, *refs
-):
+def main_kernel(rows_mesh, cols, tile_ref, table_ref, buf_ref, *refs):
     raws = refs[:cols]
-    panel_ref, fields_ref, colq, rowq, siteq, gram, inv, solved, cov, sems = refs[cols:]
+    panel_ref, fields_ref, colq, rowq, siteq, gram, lower, residual, solved, sems = refs[cols:]
     row = lax.axis_index("row")
     col = lax.axis_index("col")
     grid_y = cols * CELL_Y
@@ -198,6 +197,9 @@
     start = tile_ref[0] * TILE
     root_row = start // (SITE_DEV * cols)
     blocks = TILE // BLOCK
+    sites = cols * SITE_DEV
+    chunks = sites // CHUNK
+    parts = CHUNK // LANES
     lane = lax.broadcasted_iota(jnp.int32, (8, BLOCK), 1)
     sub = lax.broadcasted_iota(jnp.int32, (8, BLOCK), 0)
 
@@ -242,92 +244,88 @@
 
         lax.fori_loop(j * BLOCK // 16, TILE // 16, tile_step, 0)
 
+    def copy_out(b, part):
+        there = slice(b * BLOCK % width, b * BLOCK % width + BLOCK)
+        return pltpu.make_async_copy(
+            solved.at[at(b), part], panel_ref.at[there, part], sems.at[b]
+        )
+
+    own = None
     for k in range(blocks):
         diagonal = []
         for i in range(BLOCK // 8):
             values = gram[k * BLOCK + 8 * i : k * BLOCK + 8 * i + 8, at(k)]
             nug = jnp.broadcast_to(rowq[QUANT, k : k + 1, :], (8, BLOCK))
             diagonal.append(values + jnp.where(lane - 8 * i == sub, nug, 0.0))
-        own = inverse_factor(diagonal)
-        inv[at(k), at(k)] = own
+
+        def panel_chunk(ch, k=k, own=own):
+            part = slice(ch * CHUNK, (ch + 1) * CHUNK)
+            past = None
+            if k > 0:
+                solved[at(k - 1), part] = dot(own, residual[:, part])
+                past = dot(lower[at(k), : k * BLOCK], solved[: k * BLOCK, part])
+            for p in range(parts):
+                line = ch * parts + p
+                lines = [
+                    jnp.broadcast_to(siteq[q, line : line + 1, :], (8, LANES))
+                    for q in range(QUANT)
+                ]
+                for t in range(BLOCK // 8):
+                    rows = slice(k * BLOCK + 8 * t, k * BLOCK + 8 * t + 8)
+                    value = covariance([colq[q, rows, :] for q in range(QUANT)], lines)
+                    if past is not None:
+                        value = value - past[8 * t : 8 * t + 8, p * LANES : (p + 1) * LANES]
+                    residual[8 * t : 8 * t + 8, line * LANES : (line + 1) * LANES] = value
+
+        def beside(m, panel_chunk=panel_chunk):
+            steps = BLOCK // 8
+            for ch in range(chunks):
+                if ch * steps // chunks == m:
+                    panel_chunk(ch)
+
+        own = inverse_factor(diagonal, beside)
         if k > 0:
-            inv[at(k), : k * BLOCK] = dot(own, inv[at(k), : k * BLOCK])
+
+            @pl.when(col == (k - 1) * BLOCK // width)
+            def _(k=k):
+                copy_out(k - 1, slice(None)).start()
+
+        offset = start + k * BLOCK - row * sites
+
+        @pl.when((offset >= 0) & (offset < sites))
+        def _(k=k, offset=offset):
+            for i in range(BLOCK // 8):
+                nug = jnp.broadcast_to(rowq[QUANT, k : k + 1, :], (8, LANES))
+                here = pl.ds(pl.multiple_of(offset, LANES), LANES)
+                rows = slice(8 * i, 8 * i + 8)
+                residual[rows, here] = residual[rows, here] + jnp.where(
+                    lane - 8 * i == sub, nug, 0.0
+                )
+
         if k + 1 < blocks:
             rest = slice((k + 1) * BLOCK, TILE)
-            lower = dot_t(gram[rest, at(k)], own)
+            part = dot_t(gram[rest, at(k)], own)
+            lower[rest, at(k)] = part
             for i in range(k + 1, blocks):
-                mine = lower[(i - k - 1) * BLOCK : (i - k) * BLOCK, :]
+                mine = part[(i - k - 1) * BLOCK : (i - k) * BLOCK, :]
                 upto = slice((k + 1) * BLOCK, (i + 1) * BLOCK)
-                gram[at(i), upto] = gram[at(i), upto] - dot_t(mine, lower[: (i - k) * BLOCK, :])
-            if k > 0:
-                inv[rest, : k * BLOCK] = inv[rest, : k * BLOCK] - dot(
-                    lower, inv[at(k), : k * BLOCK]
-                )
-            inv[rest, at(k)] = -dot(lower, own)
-
-    first = pl.multiple_of(col * width, width)
-    depth = (col + 1) * (width // BLOCK)
-    chunks = cols * SITE_DEV // CHUNK
-    parts = CHUNK // LANES
-    eye = lax.broadcasted_iota(jnp.int32, (BLOCK, LANES), 0) == lax.broadcasted_iota(
-        jnp.int32, (BLOCK, LANES), 1
-    )
-
-    def chunk_step(ch, carry):
-        lines = [
-            [
-                jnp.broadcast_to(siteq[q, pl.ds(ch * parts + p, 1), :], (8, LANES))
-                for q in range(QUANT)
-            ]
-            for p in range(parts)
-        ]
-        here = pl.multiple_of(ch * CHUNK, CHUNK)
-
-        def depth_step(kb, carry):
-            base = pl.multiple_of(kb * BLOCK, BLOCK)
-            for t in range(BLOCK // 8):
-                pick = [colq[q, pl.ds(base + 8 * t, 8), :] for q in range(QUANT)]
-                for p in range(parts):
-                    cov[8 * t : 8 * t + 8, p * LANES : (p + 1) * LANES] = covariance(
-                        pick, lines[p]
-                    )
-            for p in range(parts):
-                same = start + base == row * (cols * SITE_DEV) + here + p * LANES
-
-                @pl.when(same)
-                def _(p=p):
-                    nug = jnp.broadcast_to(rowq[QUANT, pl.ds(kb, 1), :], (BLOCK, LANES))
-                    part = slice(p * LANES, (p + 1) * LANES)
-                    cov[:, part] = cov[:, part] + jnp.where(eye, nug, 0.0)
-
-            product = dot(inv[pl.ds(first, width), pl.ds(base, BLOCK)], cov[...])
-
-            @pl.when(kb == 0)
-            def _():
-                solved[:, pl.ds(here, CHUNK)] = product
-
-            @pl.when(kb > 0)
-            def _():
-                solved[:, pl.ds(here, CHUNK)] = solved[:, pl.ds(here, CHUNK)] + product
-
-            return carry
-
-        lax.fori_loop(0, depth, depth_step, 0)
-        pltpu.make_async_copy(
-            solved.at[:, pl.ds(here, CHUNK)], panel_ref.at[:, pl.ds(here, CHUNK)], sems.at[ch]
-        ).start()
-        return carry
-
-    lax.fori_loop(0, chunks, chunk_step, 0)
-
-    def finish(ch, carry):
-        here = pl.multiple_of(ch * CHUNK, CHUNK)
-        pltpu.make_async_copy(
-            solved.at[:, pl.ds(here, CHUNK)], panel_ref.at[:, pl.ds(here, CHUNK)], sems.at[ch]
-        ).wait()
-        return carry
-
-    lax.fori_loop(0, chunks, finish, 0)
+                gram[at(i), upto] = gram[at(i), upto] - dot_t(mine, part[: (i - k) * BLOCK, :])
+
+    last = blocks - 1
+    mine = col == last * BLOCK // width
+    for ch in range(chunks):
+        part = slice(ch * CHUNK, (ch + 1) * CHUNK)
+        solved[at(last), part] = dot(own, residual[:, part])
+
+        @pl.when(mine)
+        def _(part=part):
+            copy_out(last, part).start()
+
+    for b in range(blocks):
+
+        @pl.when(col == b * BLOCK // width)
+        def _(b=b):
+            copy_out(b, slice(None)).wait()
 
 
 def body(offsets, site_cell, estimates, panel_tile):
@@ -371,9 +369,9 @@
             pltpu.VMEM((QUANT, cols * SITE_ROWS, LANES), jnp.float32),
             pltpu.VMEM((TILE, TILE), jnp.float32),
             pltpu.VMEM((TILE, TILE), jnp.float32),
-            pltpu.VMEM((width, sites), jnp.float32),
-            pltpu.VMEM((BLOCK, CHUNK), jnp.float32),
-            pltpu.SemaphoreType.DMA((sites // CHUNK,)),
+            pltpu.VMEM((BLOCK, sites), jnp.float32),
+            pltpu.VMEM((TILE, sites), jnp.float32),
+            pltpu.SemaphoreType.DMA((TILE // BLOCK,)),
         ],
         compiler_params=pltpu.CompilerParams(vmem_limit_bytes=40 * 1024 * 1024),
     )(panel_tile, buf, buf, *raws)

time: 61.6 us -> 48.3 us (0.78)
  the two profiles are of different devices: /device:TPU:1 before, /device:TPU:0 now
where the time goes in v1:
time: 48.3 us; the launch traced here: 47.8 us
  Pallas kernels  26.6 us (55%)
  starting transfers between devices  10.5 us (22%)
  waiting for transfers between devices  7.91 us (16%)
  between operations  1.46 us (3%)
  other arithmetic  0.74 us (2%)
  local copies, waits for them, and re-layouts  0.7 us (1%)
    pallas_call x1, Pallas kernels, body(): pl.pallas_call(functools.partial(main_kernel, rows_mesh, cols), out_shape...  25.1 us
    ppermute x5, starting transfers between devices, body(): buf = buf + lax.ppermute(buf, ('row', 'col'), pairs)  10.5 us
    ppermute x5, waiting for transfers between devices, body(): buf = buf + lax.ppermute(buf, ('row', 'col'), pairs)  7.91 us
    pallas_call x1, Pallas kernels, body(): pl.pallas_call(functools.partial(pack_kernel, cols), out_shape=(jax.Shape...  1.46 us
  transfers between devices with their start and end apart: 6, of which 5 were waited for; matrix products, arithmetic and copies ran while one was open for 0% of the time, Pallas kernels for 0%

profile of v1, /device:TPU:0, one launch (start us, length us, event | category | flops | bytes accessed | tf_op | source)
XLA Modules:
  0.0 47.8 jit_solution(7872495120835728022)
XLA Ops:
  1.3 1.5 %shard_map.59 = (f32[24,128]{1,0:T(8,128)}, f32[28,128]{1,0:T(8,128)}) custom-call(s32[1]{0:T(128)S(6)} %copy.6.tile_ref, f32[4,4,4]{2,1,0:T(4,128)} %est_ref.1, f32[2,1024]{1,0:T(2,128)} %offsets_ref.1, s32[1,1024]{1,0:T(1,128)} %bitcast.1), custom_call_target="tpu_custom_call" | custom-call | tf_op jit(solution)/shard_map/pallas_call | solution.py:339
  2.7 0.5 %collective-permute-start = (f32[28,128]{1,0:T(8,128)}, f32[28,128]{1,0:T(8,128)S(1)}, u32[]{:S(2)}, u32[]{:S(2)}) collective-permute-start(f32[28,128]{1,0:T(8,128)} %get-tuple-element.4), channel_id=1, source_target_pairs={{0,1},{1,0},{2,3},{3,2},{4,5},{5,4},{6,7},{7,6},{8,9},{9,8},{10,11... | collective-permute-start | bytes 43016 | tf_op jit(solution)/shard_map/ppermute | solution.py:354
  3.2 1.0 %collective-permute-done = f32[28,128]{1,0:T(8,128)S(1)} collective-permute-done((f32[28,128]{1,0:T(8,128)}, f32[28,128]{1,0:T(8,128)S(1)}, u32[]{:S(2)}, u32[]{:S(2)}) %collective-permute-start) | collective-permute-done | bytes 14368 | tf_op jit(solution)/shard_map/ppermute | solution.py:354
  4.3 0.7 %add.15 = f32[28,128]{1,0:T(8,128)S(1)} add(f32[28,128]{1,0:T(8,128)} %get-tuple-element.4, f32[28,128]{1,0:T(8,128)S(1)} %collective-permute-done) | non-fusion elementwise | flops 3584 | bytes 43008 | tf_op jit(solution)/shard_map/add | solution.py:354
  5.0 2.8 %collective-permute-start.1 = (f32[28,128]{1,0:T(8,128)S(1)}, f32[28,128]{1,0:T(8,128)S(1)}, u32[]{:S(2)}, u32[]{:S(2)}) collective-permute-start(f32[28,128]{1,0:T(8,128)S(1)} %add.15), channel_id=1, source_target_pairs={{0,2},{1,3},{2,0},{3,1},{4,6},{5,7},{6,4},{7,5},{8,10},{9,11},{10,... | collective-permute-start | bytes 43016 | tf_op jit(solution)/shard_map/ppermute | solution.py:354
  7.8 1.7 %collective-permute-done.1 = f32[28,128]{1,0:T(8,128)S(1)} collective-permute-done((f32[28,128]{1,0:T(8,128)S(1)}, f32[28,128]{1,0:T(8,128)S(1)}, u32[]{:S(2)}, u32[]{:S(2)}) %collective-permute-start.1) | collective-permute-done | bytes 14368 | tf_op jit(solution)/shard_map/ppermute | solution.py:354
  9.5 2.1 %collective-permute-start.2 = (f32[28,128]{1,0:T(8,128)S(1)}, f32[28,128]{1,0:T(8,128)S(1)}, u32[]{:S(2)}, u32[]{:S(2)}) collective-permute-start(f32[28,128]{1,0:T(8,128)S(1)} %add.16), channel_id=1, source_target_pairs={{0,4},{1,5},{2,6},{3,7},{4,0},{5,1},{6,2},{7,3},{8,12},{9,13},{10,... | collective-permute-start | bytes 43016 | tf_op jit(solution)/shard_map/ppermute | solution.py:354
  11.6 1.7 %collective-permute-done.2 = f32[28,128]{1,0:T(8,128)S(1)} collective-permute-done((f32[28,128]{1,0:T(8,128)S(1)}, f32[28,128]{1,0:T(8,128)S(1)}, u32[]{:S(2)}, u32[]{:S(2)}) %collective-permute-start.2) | collective-permute-done | bytes 14368 | tf_op jit(solution)/shard_map/ppermute | solution.py:354
  13.3 2.1 %collective-permute-start.3 = (f32[28,128]{1,0:T(8,128)S(1)}, f32[28,128]{1,0:T(8,128)S(1)}, u32[]{:S(2)}, u32[]{:S(2)}) collective-permute-start(f32[28,128]{1,0:T(8,128)S(1)} %add.17), channel_id=1, source_target_pairs={{0,8},{1,9},{2,10},{3,11},{4,12},{5,13},{6,14},{7,15},{8,0},{9,1},... | collective-permute-start | bytes 43016 | tf_op jit(solution)/shard_map/ppermute | solution.py:354
  15.4 1.7 %collective-permute-done.3 = f32[28,128]{1,0:T(8,128)S(1)} collective-permute-done((f32[28,128]{1,0:T(8,128)S(1)}, f32[28,128]{1,0:T(8,128)S(1)}, u32[]{:S(2)}, u32[]{:S(2)}) %collective-permute-start.3) | collective-permute-done | bytes 14368 | tf_op jit(solution)/shard_map/ppermute | solution.py:354
  17.1 3.0 %collective-permute-start.4 = (f32[28,128]{1,0:T(8,128)S(1)}, f32[28,128]{1,0:T(8,128)S(1)}, u32[]{:S(2)}, u32[]{:S(2)}) collective-permute-start(f32[28,128]{1,0:T(8,128)S(1)} %add.18), channel_id=1, source_target_pairs={{0,16},{1,17},{2,18},{3,19},{4,20},{5,21},{6,22},{7,23},{8,24},{9,... | collective-permute-start | bytes 43016 | tf_op jit(solution)/shard_map/ppermute | solution.py:354
  20.2 0.0 collective-permute-start.5
  20.2 1.7 %collective-permute-done.4 = f32[28,128]{1,0:T(8,128)S(1)} collective-permute-done((f32[28,128]{1,0:T(8,128)S(1)}, f32[28,128]{1,0:T(8,128)S(1)}, u32[]{:S(2)}, u32[]{:S(2)}) %collective-permute-start.4) | collective-permute-done | bytes 14368 | tf_op jit(solution)/shard_map/ppermute | solution.py:354
  21.9 0.0 collective-permute-done.5.refs_1_
  21.9 0.0 copy-start
  21.9 0.7 %copy-done = f32[24,128]{1,0:T(8,128)S(1)} copy-done((f32[24,128]{1,0:T(8,128)S(1)}, f32[24,128]{1,0:T(8,128)}, u32[]{:S(2)}) %copy-start) | copy-done | bytes 12312
  22.6 25.1 %shard_map.60 = (f32[256,2048]{1,0:T(8,128)}, f32[4,1024]{1,0:T(4,128)}) custom-call(s32[1]{0:T(128)S(6)} %copy.6.tile_ref, f32[28,128]{1,0:T(8,128)S(1)} %add.19.table_ref.buf_ref, f32[28,128]{1,0:T(8,128)S(1)} %add.19.table_ref.buf_ref, f32[24,128]{1,0:T(8,128)S(1)} %copy-done, f32[24,128]{1,0:T(8,128)S(1)} %collective-permute-done.5.refs_1_), custom_call_target="tpu_custom_call" | custom-call | tf_op jit(solution)/shard_map/pallas_call | solution.py:358
  (4 shorter events, 0.0 us)
Async XLA Ops:
  2.7 1.5 %collective-permute-start = (f32[28,128]{1,0:T(8,128)}, f32[28,128]{1,0:T(8,128)S(1)}, u32[]{:S(2)}, u32[]{:S(2)}) collective-permute-start(f32[28,128]{1,0:T(8,128)} %get-tuple-element.4), channel_id=1, source_target_pairs={{0,1},{1,0},{2,3},{3,2},{4,5},{5,4},{6,7},{7,6},{8,9},{9,8},{10,11... | collective-permute-start | bytes 43016 | tf_op jit(solution)/shard_map/ppermute | solution.py:354
  5.0 4.5 %collective-permute-start.1 = (f32[28,128]{1,0:T(8,128)S(1)}, f32[28,128]{1,0:T(8,128)S(1)}, u32[]{:S(2)}, u32[]{:S(2)}) collective-permute-start(f32[28,128]{1,0:T(8,128)S(1)} %add.15), channel_id=1, source_target_pairs={{0,2},{1,3},{2,0},{3,1},{4,6},{5,7},{6,4},{7,5},{8,10},{9,11},{10,... | collective-permute-start | bytes 43016 | tf_op jit(solution)/shard_map/ppermute | solution.py:354
  9.5 3.8 %collective-permute-start.2 = (f32[28,128]{1,0:T(8,128)S(1)}, f32[28,128]{1,0:T(8,128)S(1)}, u32[]{:S(2)}, u32[]{:S(2)}) collective-permute-start(f32[28,128]{1,0:T(8,128)S(1)} %add.16), channel_id=1, source_target_pairs={{0,4},{1,5},{2,6},{3,7},{4,0},{5,1},{6,2},{7,3},{8,12},{9,13},{10,... | collective-permute-start | bytes 43016 | tf_op jit(solution)/shard_map/ppermute | solution.py:354
  13.3 3.8 %collective-permute-start.3 = (f32[28,128]{1,0:T(8,128)S(1)}, f32[28,128]{1,0:T(8,128)S(1)}, u32[]{:S(2)}, u32[]{:S(2)}) collective-permute-start(f32[28,128]{1,0:T(8,128)S(1)} %add.17), channel_id=1, source_target_pairs={{0,8},{1,9},{2,10},{3,11},{4,12},{5,13},{6,14},{7,15},{8,0},{9,1},... | collective-permute-start | bytes 43016 | tf_op jit(solution)/shard_map/ppermute | solution.py:354
  17.1 4.8 %collective-permute-start.4 = (f32[28,128]{1,0:T(8,128)S(1)}, f32[28,128]{1,0:T(8,128)S(1)}, u32[]{:S(2)}, u32[]{:S(2)}) collective-permute-start(f32[28,128]{1,0:T(8,128)S(1)} %add.18), channel_id=1, source_target_pairs={{0,16},{1,17},{2,18},{3,19},{4,20},{5,21},{6,22},{7,23},{8,24},{9,... | collective-permute-start | bytes 43016 | tf_op jit(solution)/shard_map/ppermute | solution.py:354
  20.2 1.7 %collective-permute-start.5 = (f32[24,128]{1,0:T(8,128)}, f32[24,128]{1,0:T(8,128)S(1)}, u32[]{:S(2)}, u32[]{:S(2)}) collective-permute-start(f32[24,128]{1,0:T(8,128)} %get-tuple-element.5.refs_0_), channel_id=1, source_target_pairs={{0,1},{1,0},{2,3},{3,2},{4,5},{5,4},{6,7},{7,6},{8,9},{9,8},{10,11... | collective-permute-start | bytes 36872 | tf_op jit(solution)/shard_map/ppermute | solution.py:350
  21.9 0.7 %copy-start = (f32[24,128]{1,0:T(8,128)S(1)}, f32[24,128]{1,0:T(8,128)}, u32[]{:S(2)}) copy-start(f32[24,128]{1,0:T(8,128)} %get-tuple-element.5.refs_0_) | copy-start | bytes 36868

commit v2 on v1

v2 whole, which is shorter than its diff:
```python
import functools

import jax
import jax.numpy as jnp
from jax import lax
from jax.experimental import pallas as pl
from jax.experimental.pallas import tpu as pltpu
from jax.sharding import PartitionSpec as P

SITE_DEV = 1024
TILE = 512
CELL_X = 4
CELL_Y = 4
RADIUS = 2

spread_cells = 1.5
nugget_share = 0.5
range_shift = -0.7

LANES = 128
BLOCK = 128
FIELDS = 4
SITE_ROWS = SITE_DEV // LANES
TILE_ROWS = TILE // LANES
RAW = 3 * SITE_ROWS
HEAD = 3 * TILE_ROWS
CHUNK = 256
QUANT = 5

HIGHEST = lax.Precision.HIGHEST


def dot(a, b):
    return jnp.dot(a, b, precision=HIGHEST, preferred_element_type=jnp.float32)


def dot_t(a, b):
    return lax.dot_general(
        a, b, (((1,), (1,)), ((), ())), precision=HIGHEST, preferred_element_type=jnp.float32
    )


def pack_kernel(cols, tile_ref, est_ref, offsets_ref, cell_ref, out_ref):
    row = lax.axis_index("row")
    col = lax.axis_index("col")
    for j in range(SITE_ROWS):
        part = slice(j * LANES, (j + 1) * LANES)
        out_ref[j : j + 1, :] = offsets_ref[0:1, part]
        out_ref[SITE_ROWS + j : SITE_ROWS + j + 1, :] = offsets_ref[1:2, part]
        out_ref[2 * SITE_ROWS + j : 2 * SITE_ROWS + j + 1, :] = cell_ref[0:1, part].astype(
            jnp.float32
        )
    start = tile_ref[0] * TILE
    root = start // SITE_DEV
    first = (start - root * SITE_DEV) // LANES
    mine = row * cols + col == root
    for q in range(3):
        rows = out_ref[pl.ds(q * SITE_ROWS + first, TILE_ROWS), :]
        there = RAW + q * TILE_ROWS
        out_ref[there : there + TILE_ROWS, :] = jnp.where(mine, rows, 0.0)
    grid_y = cols * CELL_Y
    lane = lax.broadcasted_iota(jnp.int32, (1, LANES), 1) - col * CELL_Y
    terms = []
    for f in range(FIELDS):
        for a in range(CELL_X):
            line = jnp.zeros((1, LANES), jnp.float32)
            for b in range(CELL_Y):
                line = jnp.where(
                    lane == (f * CELL_X + a) * grid_y + b, est_ref[f, a, b], line
                )
            terms.append(line)
    while len(terms) > 1:
        terms = [x + y for x, y in zip(terms[::2], terms[1::2])]
    count = out_ref.shape[0] - RAW - HEAD
    index = lax.broadcasted_iota(jnp.int32, (count, LANES), 0)
    out_ref[RAW + HEAD :, :] = jnp.where(
        index == row, jnp.broadcast_to(terms[0], (count, LANES)), 0.0
    )


def smooth(raw, block_row, table_ref, rows_mesh, grid_y):
    off_x, off_y, cell = raw
    total_x = CELL_X * rows_mesh
    cell_x = jnp.floor((cell + 0.5) / grid_y)
    cell_y = cell - cell_x * grid_y
    loc_x = cell_x + off_x
    loc_y = cell_y + off_y
    weight_y = []
    for b in range(grid_y):
        dist = loc_y - (b + 0.5)
        value = jnp.exp(-dist * dist / (2.0 * spread_cells * spread_cells))
        weight_y.append(jnp.where(jnp.abs(cell_y - b) <= RADIUS, value, 0.0))
    sum_y = functools.reduce(jnp.add, weight_y)
    numer = [None] * FIELDS
    sum_x = None
    for a in range(CELL_X - RADIUS, 2 * CELL_X + RADIUS):
        coord = (block_row - 1) * CELL_X + a
        near = block_row - 1 + a // CELL_X
        line = HEAD + jnp.clip(near, 0, rows_mesh - 1)
        coord_f = coord.astype(jnp.float32)
        dist = loc_x - coord_f - 0.5
        value = jnp.exp(-dist * dist / (2.0 * spread_cells * spread_cells))
        inside = (coord >= 0) & (coord < total_x)
        reach = jnp.where(inside, float(RADIUS), -1.0)
        weight = jnp.where(jnp.abs(cell_x - coord_f) <= reach, value, 0.0)
        sum_x = weight if sum_x is None else sum_x + weight
        for f in range(FIELDS):
            base = (f * CELL_X + a % CELL_X) * grid_y
            inner = None
            for b in range(grid_y):
                term = table_ref[line, base + b] * weight_y[b]
                inner = term if inner is None else inner + term
            term = inner * weight
            numer[f] = term if numer[f] is None else numer[f] + term
    denom = sum_x * sum_y
    return [n / denom for n in numer], loc_x, loc_y


def quantities(fields, loc_x, loc_y, total_x):
    first = jnp.exp(2.0 * (fields[0] + range_shift))
    second = jnp.exp(2.0 * (fields[1] + range_shift))
    cosine = jnp.cos(fields[2])
    sine = jnp.sin(fields[2])
    m_a = (cosine * cosine * first + sine * sine * second) * (1.0 / 6.0)
    m_b = (sine * sine * first + cosine * cosine * second) * (1.0 / 6.0)
    m_c = (cosine * sine * (first - second)) * (1.0 / 6.0)
    return [m_a, m_b, m_c, loc_x / total_x, loc_y / total_x]


def log_root(fields):
    return fields[0] + fields[1] + 2.0 * range_shift


def site_scale(fields):
    return jnp.exp(fields[3] + 0.5 * log_root(fields)) * (3.0**-0.5)


def scaled_nugget(fields):
    return (3.0 * nugget_share) * jnp.exp(-log_root(fields))


def covariance(cols, rows, scale=None):
    m_aa = cols[0] + rows[0]
    m_bb = cols[1] + rows[1]
    m_ab = cols[2] + rows[2]
    diff_x = cols[3] - rows[3]
    diff_y = cols[4] - rows[4]
    inv_root = lax.rsqrt(m_aa * m_bb - m_ab * m_ab)
    form = diff_x * (m_bb * diff_x - m_ab * diff_y) + diff_y * (m_aa * diff_y - m_ab * diff_x)
    form = jnp.maximum(form, 1e-36)
    dist = form * lax.rsqrt(form) * inv_root
    value = (inv_root + inv_root * dist) * jnp.exp(-dist)
    return value if scale is None else value * scale


def halves(values):
    high = values.astype(jnp.bfloat16)
    return high, (values - high.astype(jnp.float32)).astype(jnp.bfloat16)


def left_parts(values):
    high, low = halves(values)
    return jnp.concatenate([high, high, low], axis=1)


def right_parts(values):
    high, low = halves(values)
    return jnp.concatenate([high, low, high], axis=0)


def dot_parts(left, right):
    return jnp.dot(left, right, preferred_element_type=jnp.float32)


def lane_copy(values, lane):
    index = jnp.full(values.shape, lane, jnp.int32)
    return jnp.take_along_axis(values, index, axis=1)


def row_copy(values, row):
    return jnp.broadcast_to(values[row : row + 1, :], values.shape)


def inverse_factor(rows, beside):
    steps = BLOCK // 8
    lane = lax.broadcasted_iota(jnp.int32, (8, BLOCK), 1)
    sub = lax.broadcasted_iota(jnp.int32, (8, BLOCK), 0)
    rows = list(rows)
    out = [None] * steps
    for m in range(steps):
        at = 8 * m
        pivots = (lane >= at) & (lane < at + 8)
        column = [lane_copy(rows[m], at + c) for c in range(8)]
        block = jnp.where(lane - at == sub, 1.0, jnp.where(pivots, 0.0, rows[m]))
        solved = jnp.zeros((8, BLOCK), jnp.float32)
        pairs = []
        for c in range(0, 8, 2):
            p = row_copy(column[c], c)
            r = row_copy(column[c + 1], c)
            q = row_copy(column[c + 1], c + 1)
            det = p * q - r * r
            inv = 1.0 / det
            both = (sub == c) | (sub == c + 1)
            first = jnp.where(both, 0.0, column[c])
            second = jnp.where(both, 0.0, column[c + 1])
            left = q * first - r * second
            right = p * second - r * first
            upper = row_copy(block, c)
            under = row_copy(block, c + 1)
            solved = jnp.where(sub == c, upper * lax.rsqrt(p), solved)
            solved = jnp.where(
                sub == c + 1, (p * under - r * upper) * lax.rsqrt(p * det), solved
            )
            pairs.append((p, r, q, inv))
            if c + 2 < 8:
                left_inv = left * inv
                right_inv = right * inv
                for j in range(c + 2, 8):
                    a = row_copy(column[j], c)
                    b = row_copy(column[j], c + 1)
                    if j < c + 4:
                        column[j] = column[j] - (left * a + right * b) * inv
                    else:
                        column[j] = (column[j] - left_inv * a) - right_inv * b
                block = (block - left_inv * upper) - right_inv * under
            else:
                block = block - (left * upper + right * under) * inv
        out[m] = solved
        beside(m)
        if m == steps - 1:
            break
        lines = []
        for h, (p, r, q, inv) in enumerate(pairs):
            upper = row_copy(block, 2 * h)
            under = row_copy(block, 2 * h + 1)
            lines.append((q * upper - r * under) * inv)
            lines.append((p * under - r * upper) * inv)
        term = [lane_copy(rows[m + 1], at + c) * lines[c] for c in range(8)]
        total = [None] * steps
        total[m + 1] = ((term[0] + term[1]) + (term[2] + term[3])) + (
            (term[4] + term[5]) + (term[6] + term[7])
        )
        for c in range(8):
            for i in range(m + 2, steps):
                term = lane_copy(rows[i], at + c) * lines[c]
                total[i] = term if c == 0 else total[i] + term
        for i in range(m + 1, steps):
            rows[i] = jnp.where(pivots, 0.0, rows[i]) - total[i]
    result = jnp.concatenate(out, axis=0)
    r = lax.broadcasted_iota(jnp.int32, (BLOCK, BLOCK), 0)
    c = lax.broadcasted_iota(jnp.int32, (BLOCK, BLOCK), 1)
    return jnp.where(c <= r, result, 0.0)


def at(block):
    return slice(block * BLOCK, (block + 1) * BLOCK)


def main_kernel(rows_mesh, cols, tile_ref, table_ref, buf_ref, *refs):
    packs = refs[:cols]
    (
        panel_ref,
        fields_ref,
        raws,
        colq,
        rowq,
        siteq,
        gram,
        lower,
        left,
        right,
        residual,
        solved,
        raw_sems,
        sems,
    ) = refs[cols:]
    row = lax.axis_index("row")
    col = lax.axis_index("col")
    grid_y = cols * CELL_Y
    total_x = float(CELL_X * rows_mesh)
    width = TILE // cols
    start = tile_ref[0] * TILE
    root_row = start // (SITE_DEV * cols)
    blocks = TILE // BLOCK
    sites = cols * SITE_DEV
    chunks = sites // CHUNK
    parts = CHUNK // LANES
    steps = BLOCK // 8
    lane = lax.broadcasted_iota(jnp.int32, (8, BLOCK), 1)
    sub = lax.broadcasted_iota(jnp.int32, (8, BLOCK), 0)

    def raw_copy(k):
        return pltpu.make_async_copy(packs[k].at[0:RAW], raws.at[k], raw_sems.at[k])

    for k in range(cols):
        raw_copy(k).start()

    raw = [buf_ref[q * TILE_ROWS : (q + 1) * TILE_ROWS, :] for q in range(3)]
    fields, loc_x, loc_y = smooth(raw, root_row, table_ref, rows_mesh, grid_y)
    quant = quantities(fields, loc_x, loc_y, total_x)
    for q in range(QUANT):
        rowq[q, :, :] = quant[q]
    rowq[QUANT, :, :] = scaled_nugget(fields)
    for k in range(cols):
        raw_copy(k).wait()

    def panel_columns(g):
        pad = jnp.zeros((8 - QUANT, LANES), jnp.float32)
        turned = jnp.transpose(
            jnp.concatenate([quant[q][g : g + 1, :] for q in range(QUANT)] + [pad], axis=0)
        )
        for q in range(QUANT):
            colq[q, g * LANES : (g + 1) * LANES, :] = jnp.broadcast_to(
                turned[:, q : q + 1], (LANES, LANES)
            )

    def panel_gram(i, j):
        lines = [jnp.broadcast_to(rowq[q, j : j + 1, :], (8, LANES)) for q in range(QUANT)]
        for t in range(steps):
            rows = slice(i * BLOCK + 8 * t, i * BLOCK + 8 * t + 8)
            gram[rows, at(j)] = covariance([colq[q, rows, :] for q in range(QUANT)], lines)

    def site_rows():
        raw = [
            jnp.concatenate(
                [raws[k, q * SITE_ROWS : (q + 1) * SITE_ROWS, :] for k in range(cols)], axis=0
            )
            for q in range(3)
        ]
        fields, loc_x, loc_y = smooth(raw, row, table_ref, rows_mesh, grid_y)
        for f in range(FIELDS):
            for j in range(SITE_ROWS):
                fields_ref[f : f + 1, j * LANES : (j + 1) * LANES] = fields[f][j : j + 1, :]
        values = quantities(fields, loc_x, loc_y, total_x) + [site_scale(fields)]
        for k in range(cols):
            member = pl.multiple_of(jnp.bitwise_xor(col, k) * SITE_ROWS, 8)
            for q in range(QUANT + 1):
                siteq[q, pl.ds(member, SITE_ROWS), :] = values[q][
                    k * SITE_ROWS : (k + 1) * SITE_ROWS, :
                ]

    def copy_out(b, part):
        there = slice(b * BLOCK % width, b * BLOCK % width + BLOCK)
        return pltpu.make_async_copy(
            solved.at[at(b), part], panel_ref.at[there, part], sems.at[b]
        )

    def wide(j):
        return slice(3 * j * BLOCK, 3 * (j + 1) * BLOCK)

    def solve_chunk(k, own_parts, part):
        values = dot_parts(own_parts, right_parts(residual[:, part]))
        solved[at(k), part] = values
        return values

    def panel_chunk(ch, k, own_parts):
        part = slice(ch * CHUNK, (ch + 1) * CHUNK)
        past = None
        if k > 0:
            values = solve_chunk(k - 1, own_parts, part)
            right[wide(k - 1), part] = right_parts(values)
            past = dot_parts(left[at(k), : 3 * k * BLOCK], right[: 3 * k * BLOCK, part])
        for p in range(parts):
            line = ch * parts + p
            lines = [
                jnp.broadcast_to(siteq[q, line : line + 1, :], (8, LANES))
                for q in range(QUANT + 1)
            ]
            for t in range(steps):
                rows = slice(k * BLOCK + 8 * t, k * BLOCK + 8 * t + 8)
                value = covariance(
                    [colq[q, rows, :] for q in range(QUANT)], lines[:QUANT], lines[QUANT]
                )
                if past is not None:
                    value = value - past[8 * t : 8 * t + 8, p * LANES : (p + 1) * LANES]
                residual[8 * t : 8 * t + 8, line * LANES : (line + 1) * LANES] = value

    def lower_block(i, k, own):
        values = dot_t(gram[at(i), at(k)], own)
        lower[at(i), at(k)] = values
        left[at(i), wide(k)] = left_parts(values)

    def update_block(i, j, k):
        gram[at(i), at(j)] = gram[at(i), at(j)] - dot_t(lower[at(i), at(k)], lower[at(j), at(k)])

    panel_columns(0)
    panel_gram(0, 0)
    own = None
    for k in range(blocks):
        diagonal = []
        for i in range(steps):
            values = gram[k * BLOCK + 8 * i : k * BLOCK + 8 * i + 8, at(k)]
            nug = jnp.broadcast_to(rowq[QUANT, k : k + 1, :], (8, BLOCK))
            diagonal.append(values + jnp.where(lane - 8 * i == sub, nug, 0.0))
        own_parts = None if own is None else left_parts(own)

        def beside(m, k=k, own=own, own_parts=own_parts):
            if m == 0 and k == 0:
                site_rows()
            if k == 0 and 0 < m < blocks:
                panel_columns(m)
                for j in range(m + 1):
                    panel_gram(m, j)
            if m == 0 and k > 0:
                for i in range(k + 1, blocks):
                    lower_block(i, k - 1, own)
                    for j in range(k, i + 1):
                        update_block(i, j, k - 1)
            for ch in range(chunks):
                if ch * steps // chunks == m:
                    panel_chunk(ch, k, own_parts)

        own = inverse_factor(diagonal, beside)
        if k + 1 < blocks:
            lower_block(k + 1, k, own)
            update_block(k + 1, k + 1, k)
        if k > 0:

            @pl.when(col == (k - 1) * BLOCK // width)
            def _(k=k):
                copy_out(k - 1, slice(None)).start()

        offset = start + k * BLOCK - row * sites

        @pl.when((offset >= 0) & (offset < sites))
        def _(k=k, offset=offset):
            line = offset // LANES
            nug = rowq[QUANT, k : k + 1, :] * siteq[QUANT, pl.ds(line, 1), :]
            here = pl.ds(pl.multiple_of(offset, LANES), LANES)
            for i in range(steps):
                rows = slice(8 * i, 8 * i + 8)
                residual[rows, here] = residual[rows, here] + jnp.where(
                    lane - 8 * i == sub, jnp.broadcast_to(nug, (8, LANES)), 0.0
                )

    last = blocks - 1
    mine = col == last * BLOCK // width
    own_parts = left_parts(own)
    for ch in range(chunks):
        part = slice(ch * CHUNK, (ch + 1) * CHUNK)
        solve_chunk(last, own_parts, part)

        @pl.when(mine)
        def _(part=part):
            copy_out(last, part).start()

    for b in range(blocks):

        @pl.when(col == b * BLOCK // width)
        def _(b=b):
            copy_out(b, slice(None)).wait()


def body(offsets, site_cell, estimates, panel_tile):
    rows_mesh = lax.axis_size("row")
    cols = lax.axis_size("col")
    devices = rows_mesh * cols
    assert FIELDS * CELL_X * CELL_Y * cols == LANES
    assert devices & (devices - 1) == 0
    vmem = pl.BlockSpec(memory_space=pltpu.VMEM)
    smem = pl.BlockSpec(memory_space=pltpu.SMEM)
    pack = pl.pallas_call(
        functools.partial(pack_kernel, cols),
        out_shape=jax.ShapeDtypeStruct((RAW + HEAD + rows_mesh, LANES), jnp.float32),
        in_specs=[smem, smem, vmem, vmem],
        out_specs=vmem,
    )(panel_tile, estimates, offsets, site_cell.reshape(1, -1))
    packs = [pack]
    buf = pack[RAW:]
    step = 1
    while step < devices:
        pairs = [(i, i ^ step) for i in range(devices)]
        if step < cols:
            sent = jnp.concatenate([pack[:RAW], buf], axis=0) if step > 1 else pack
            near = lax.ppermute(sent, ("row", "col"), pairs)
            packs.append(near)
            for k in range(1, step):
                far = lax.ppermute(packs[k], ("row", "col"), pairs)
                packs.append(far)
            buf = buf + near[RAW:]
        else:
            buf = buf + lax.ppermute(buf, ("row", "col"), pairs)
        step *= 2
    width = TILE // cols
    sites = cols * SITE_DEV
    anywhere = pl.BlockSpec(memory_space=pl.ANY)
    panel, fields = pl.pallas_call(
        functools.partial(main_kernel, rows_mesh, cols),
        out_shape=(
            jax.ShapeDtypeStruct((width, sites), jnp.float32),
            jax.ShapeDtypeStruct((FIELDS, SITE_DEV), jnp.float32),
        ),
        in_specs=[smem, smem, vmem] + [anywhere] * cols,
        out_specs=(anywhere, vmem),
        scratch_shapes=[
            pltpu.VMEM((cols, RAW, LANES), jnp.float32),
            pltpu.VMEM((QUANT, TILE, LANES), jnp.float32),
            pltpu.VMEM((QUANT + 1, TILE_ROWS, LANES), jnp.float32),
            pltpu.VMEM((QUANT + 1, cols * SITE_ROWS, LANES), jnp.float32),
            pltpu.VMEM((TILE, TILE), jnp.float32),
            pltpu.VMEM((TILE, TILE), jnp.float32),
            pltpu.VMEM((TILE, 3 * TILE), jnp.bfloat16),
            pltpu.VMEM((3 * (TILE - BLOCK), sites), jnp.bfloat16),
            pltpu.VMEM((BLOCK, sites), jnp.float32),
            pltpu.VMEM((TILE, sites), jnp.float32),
            pltpu.SemaphoreType.DMA((cols,)),
            pltpu.SemaphoreType.DMA((TILE // BLOCK,)),
        ],
        compiler_params=pltpu.CompilerParams(vmem_limit_bytes=40 * 1024 * 1024),
    )(panel_tile, buf, buf, *packs)
    return (panel, fields)


def solution(mesh):
    placed = (P(None, ("row", "col")), P(("row", "col")), P(None, "row", "col"), P())
    return jax.shard_map(
        body,
        mesh=mesh,
        in_specs=placed,
        out_specs=(P("col", "row"), P(None, ("row", "col"))),
        check_vma=False,
    )
```

time: 48.3 us -> 46.3 us (0.959)
  Pallas kernels: 26.6 us -> 24.6 us
    pallas_call x1, Pallas kernels: 25.1 us -> 23.2 us  [body(): pl.pallas_call(functools.partial(main_kernel, rows_mesh, cols), out_shape...]
    ppermute x1, waiting for transfers between devices: 0.01 us -> 1.07 us  [body(): near = lax.ppermute(sent, ('row', 'col'), pairs)]
    ppermute x5 -> x4, waiting for transfers between devices: 7.91 us -> 6.86 us  [body(): buf = buf + lax.ppermute(buf, ('row', 'col'), pairs)]
    add x5 -> x4, other arithmetic: 0.74 us -> 0.02 us  [body(): buf = buf + lax.ppermute(buf, ('row', 'col'), pairs)]
    add x0 -> x1, other arithmetic: none -> 0.72 us  [body(): buf = buf + near[RAW:]]
    ppermute x5 -> x4, starting transfers between devices: 10.5 us -> 9.99 us  [body(): buf = buf + lax.ppermute(buf, ('row', 'col'), pairs)]
    ppermute x1, starting transfers between devices: 0.01 us -> 0.49 us  [body(): near = lax.ppermute(sent, ('row', 'col'), pairs)]
  transfers between devices with their start and end apart: 6 -> 5, of which waited for: 5 -> 5; matrix products, arithmetic and copies ran while one was open for 0% -> 0% of each run, Pallas kernels for 0% -> 0%
where the time goes in v2:
time: 46.3 us; the launch traced here: 46 us
  Pallas kernels  24.6 us (53%)
  starting transfers between devices  10.5 us (23%)
  waiting for transfers between devices  7.93 us (17%)
  between operations  1.45 us (3%)
  local copies, waits for them, and re-layouts  0.75 us (2%)
  other arithmetic  0.74 us (2%)
    pallas_call x1, Pallas kernels, body(): pl.pallas_call(functools.partial(main_kernel, rows_mesh, cols), out_shape...  23.2 us
    ppermute x4, starting transfers between devices, body(): buf = buf + lax.ppermute(buf, ('row', 'col'), pairs)  9.99 us
    ppermute x4, waiting for transfers between devices, body(): buf = buf + lax.ppermute(buf, ('row', 'col'), pairs)  6.86 us
    pallas_call x1, Pallas kernels, body(): pl.pallas_call(functools.partial(pack_kernel, cols), out_shape=jax.ShapeD...  1.46 us
    ppermute x1, waiting for transfers between devices, body(): near = lax.ppermute(sent, ('row', 'col'), pairs)  1.07 us
  transfers between devices with their start and end apart: 5, of which 5 were waited for; matrix products, arithmetic and copies ran while one was open for 0% of the time, Pallas kernels for 0%

profile of v2, /device:TPU:0, one launch (start us, length us, event | category | flops | bytes accessed | tf_op | source)
XLA Modules:
  0.0 46.0 jit_solution(10153621060070948595)
XLA Ops:
  1.3 1.5 %shard_map.59.refs_0_ = f32[52,128]{1,0:T(8,128)} custom-call(s32[1]{0:T(128)S(6)} %copy.6.tile_ref, f32[4,4,4]{2,1,0:T(4,128)} %est_ref.1, f32[2,1024]{1,0:T(2,128)} %offsets_ref.1, s32[1,1024]{1,0:T(1,128)} %bitcast.1), custom_call_target="tpu_custom_call" | custom-call | tf_op jit(solution)/shard_map/pallas_call | solution.py:462
  2.7 0.5 %collective-permute-start = (f32[52,128]{1,0:T(8,128)}, f32[52,128]{1,0:T(8,128)S(1)}, u32[]{:S(2)}, u32[]{:S(2)}) collective-permute-start(f32[52,128]{1,0:T(8,128)} %shard_map.59.refs_0_), channel_id=1, source_target_pairs={{0,1},{1,0},{2,3},{3,2},{4,5},{5,4},{6,7},{7,6},{8,9},{9,8},{10,11... | collective-permute-start | bytes 79880 | tf_op jit(solution)/shard_map/ppermute | solution.py:475
  3.2 1.1 %collective-permute-done.refs_1_ = f32[52,128]{1,0:T(8,128)S(1)} collective-permute-done((f32[52,128]{1,0:T(8,128)}, f32[52,128]{1,0:T(8,128)S(1)}, u32[]{:S(2)}, u32[]{:S(2)}) %collective-permute-start) | collective-permute-done | bytes 26656 | tf_op jit(solution)/shard_map/ppermute | solution.py:475
  4.3 0.7 %slice_add_fusion = f32[28,128]{1,0:T(8,128)S(1)} fusion(f32[52,128]{1,0:T(8,128)S(1)} %collective-permute-done.refs_1_, f32[52,128]{1,0:T(8,128)} %shard_map.59.refs_0_), kind=kLoop, calls=%fused_computation | loop fusion | flops 3584 | bytes 43008 | tf_op jit(solution)/shard_map/add | solution.py:480
  5.0 2.8 %collective-permute-start.1 = (f32[28,128]{1,0:T(8,128)S(1)}, f32[28,128]{1,0:T(8,128)S(1)}, u32[]{:S(2)}, u32[]{:S(2)}) collective-permute-start(f32[28,128]{1,0:T(8,128)S(1)} %slice_add_fusion), channel_id=1, source_target_pairs={{0,2},{1,3},{2,0},{3,1},{4,6},{5,7},{6,4},{7,5},{8,10},{9,11},{10,... | collective-permute-start | bytes 43016 | tf_op jit(solution)/shard_map/ppermute | solution.py:482
  7.8 1.7 %collective-permute-done.1 = f32[28,128]{1,0:T(8,128)S(1)} collective-permute-done((f32[28,128]{1,0:T(8,128)S(1)}, f32[28,128]{1,0:T(8,128)S(1)}, u32[]{:S(2)}, u32[]{:S(2)}) %collective-permute-start.1) | collective-permute-done | bytes 14368 | tf_op jit(solution)/shard_map/ppermute | solution.py:482
  9.6 2.1 %collective-permute-start.2 = (f32[28,128]{1,0:T(8,128)S(1)}, f32[28,128]{1,0:T(8,128)S(1)}, u32[]{:S(2)}, u32[]{:S(2)}) collective-permute-start(f32[28,128]{1,0:T(8,128)S(1)} %add.16), channel_id=1, source_target_pairs={{0,4},{1,5},{2,6},{3,7},{4,0},{5,1},{6,2},{7,3},{8,12},{9,13},{10,... | collective-permute-start | bytes 43016 | tf_op jit(solution)/shard_map/ppermute | solution.py:482
  11.6 1.7 %collective-permute-done.2 = f32[28,128]{1,0:T(8,128)S(1)} collective-permute-done((f32[28,128]{1,0:T(8,128)S(1)}, f32[28,128]{1,0:T(8,128)S(1)}, u32[]{:S(2)}, u32[]{:S(2)}) %collective-permute-start.2) | collective-permute-done | bytes 14368 | tf_op jit(solution)/shard_map/ppermute | solution.py:482
  13.3 2.1 %collective-permute-start.3 = (f32[28,128]{1,0:T(8,128)S(1)}, f32[28,128]{1,0:T(8,128)S(1)}, u32[]{:S(2)}, u32[]{:S(2)}) collective-permute-start(f32[28,128]{1,0:T(8,128)S(1)} %add.17), channel_id=1, source_target_pairs={{0,8},{1,9},{2,10},{3,11},{4,12},{5,13},{6,14},{7,15},{8,0},{9,1},... | collective-permute-start | bytes 43016 | tf_op jit(solution)/shard_map/ppermute | solution.py:482
  15.4 1.7 %collective-permute-done.3 = f32[28,128]{1,0:T(8,128)S(1)} collective-permute-done((f32[28,128]{1,0:T(8,128)S(1)}, f32[28,128]{1,0:T(8,128)S(1)}, u32[]{:S(2)}, u32[]{:S(2)}) %collective-permute-start.3) | collective-permute-done | bytes 14368 | tf_op jit(solution)/shard_map/ppermute | solution.py:482
  17.1 3.0 %collective-permute-start.4 = (f32[28,128]{1,0:T(8,128)S(1)}, f32[28,128]{1,0:T(8,128)S(1)}, u32[]{:S(2)}, u32[]{:S(2)}) collective-permute-start(f32[28,128]{1,0:T(8,128)S(1)} %add.18), channel_id=1, source_target_pairs={{0,16},{1,17},{2,18},{3,19},{4,20},{5,21},{6,22},{7,23},{8,24},{9,... | collective-permute-start | bytes 43016 | tf_op jit(solution)/shard_map/ppermute | solution.py:482
  20.2 1.7 %collective-permute-done.4 = f32[28,128]{1,0:T(8,128)S(1)} collective-permute-done((f32[28,128]{1,0:T(8,128)S(1)}, f32[28,128]{1,0:T(8,128)S(1)}, u32[]{:S(2)}, u32[]{:S(2)}) %collective-permute-start.4) | collective-permute-done | bytes 14368 | tf_op jit(solution)/shard_map/ppermute | solution.py:482
  21.9 0.0 copy-start
  21.9 0.7 %copy-done = f32[52,128]{1,0:T(8,128)S(1)} copy-done((f32[52,128]{1,0:T(8,128)S(1)}, f32[52,128]{1,0:T(8,128)}, u32[]{:S(2)}) %copy-start) | copy-done | bytes 26648
  22.6 23.2 %shard_map.60 = (f32[256,2048]{1,0:T(8,128)}, f32[4,1024]{1,0:T(4,128)}) custom-call(s32[1]{0:T(128)S(6)} %copy.6.tile_ref, f32[28,128]{1,0:T(8,128)S(1)} %add.19.table_ref.buf_ref, f32[28,128]{1,0:T(8,128)S(1)} %add.19.table_ref.buf_ref, f32[52,128]{1,0:T(8,128)S(1)} %copy-done, f32[52,128]{1,0:T(8,128)S(1)} %collective-permute-done.refs_1_), custom_call_target="tpu_custom_call" | custom-call | tf_op jit(solution)/shard_map/pallas_call | solution.py:487
  (4 shorter events, 0.0 us)
Async XLA Ops:
  2.7 1.6 %collective-permute-start = (f32[52,128]{1,0:T(8,128)}, f32[52,128]{1,0:T(8,128)S(1)}, u32[]{:S(2)}, u32[]{:S(2)}) collective-permute-start(f32[52,128]{1,0:T(8,128)} %shard_map.59.refs_0_), channel_id=1, source_target_pairs={{0,1},{1,0},{2,3},{3,2},{4,5},{5,4},{6,7},{7,6},{8,9},{9,8},{10,11... | collective-permute-start | bytes 79880 | tf_op jit(solution)/shard_map/ppermute | solution.py:475
  5.0 4.5 %collective-permute-start.1 = (f32[28,128]{1,0:T(8,128)S(1)}, f32[28,128]{1,0:T(8,128)S(1)}, u32[]{:S(2)}, u32[]{:S(2)}) collective-permute-start(f32[28,128]{1,0:T(8,128)S(1)} %slice_add_fusion), channel_id=1, source_target_pairs={{0,2},{1,3},{2,0},{3,1},{4,6},{5,7},{6,4},{7,5},{8,10},{9,11},{10,... | collective-permute-start | bytes 43016 | tf_op jit(solution)/shard_map/ppermute | solution.py:482
  9.6 3.8 %collective-permute-start.2 = (f32[28,128]{1,0:T(8,128)S(1)}, f32[28,128]{1,0:T(8,128)S(1)}, u32[]{:S(2)}, u32[]{:S(2)}) collective-permute-start(f32[28,128]{1,0:T(8,128)S(1)} %add.16), channel_id=1, source_target_pairs={{0,4},{1,5},{2,6},{3,7},{4,0},{5,1},{6,2},{7,3},{8,12},{9,13},{10,... | collective-permute-start | bytes 43016 | tf_op jit(solution)/shard_map/ppermute | solution.py:482
  13.3 3.8 %collective-permute-start.3 = (f32[28,128]{1,0:T(8,128)S(1)}, f32[28,128]{1,0:T(8,128)S(1)}, u32[]{:S(2)}, u32[]{:S(2)}) collective-permute-start(f32[28,128]{1,0:T(8,128)S(1)} %add.17), channel_id=1, source_target_pairs={{0,8},{1,9},{2,10},{3,11},{4,12},{5,13},{6,14},{7,15},{8,0},{9,1},... | collective-permute-start | bytes 43016 | tf_op jit(solution)/shard_map/ppermute | solution.py:482
  17.1 4.8 %collective-permute-start.4 = (f32[28,128]{1,0:T(8,128)S(1)}, f32[28,128]{1,0:T(8,128)S(1)}, u32[]{:S(2)}, u32[]{:S(2)}) collective-permute-start(f32[28,128]{1,0:T(8,128)S(1)} %add.18), channel_id=1, source_target_pairs={{0,16},{1,17},{2,18},{3,19},{4,20},{5,21},{6,22},{7,23},{8,24},{9,... | collective-permute-start | bytes 43016 | tf_op jit(solution)/shard_map/ppermute | solution.py:482
  21.9 0.7 %copy-start = (f32[52,128]{1,0:T(8,128)S(1)}, f32[52,128]{1,0:T(8,128)}, u32[]{:S(2)}) copy-start(f32[52,128]{1,0:T(8,128)} %shard_map.59.refs_0_) | copy-start | bytes 79876

commit v3 on v2

v3 whole, which is shorter than its diff:
```python
import functools

import jax
import jax.numpy as jnp
from jax import lax
from jax.experimental import pallas as pl
from jax.experimental.pallas import tpu as pltpu
from jax.sharding import PartitionSpec as P

SITE_DEV = 1024
TILE = 512
CELL_X = 4
CELL_Y = 4
RADIUS = 2

spread_cells = 1.5
nugget_share = 0.5
range_shift = -0.7

LANES = 128
BLOCK = 128
FIELDS = 4
SITE_ROWS = SITE_DEV // LANES
TILE_ROWS = TILE // LANES
RAW = 3 * SITE_ROWS
HEAD = 3 * TILE_ROWS
CHUNK = 256
STRETCH = 4
LANE_ROWS = 14
FEATURES = 16
COPIES = 8

HIGHEST = lax.Precision.HIGHEST


def dot(a, b):
    return jnp.dot(a, b, precision=HIGHEST, preferred_element_type=jnp.float32)


def dot_t(a, b):
    return lax.dot_general(
        a, b, (((1,), (1,)), ((), ())), precision=HIGHEST, preferred_element_type=jnp.float32
    )


def pack_kernel(cols, tile_ref, est_ref, offsets_ref, cell_ref, out_ref):
    row = lax.axis_index("row")
    col = lax.axis_index("col")
    for j in range(SITE_ROWS):
        part = slice(j * LANES, (j + 1) * LANES)
        out_ref[j : j + 1, :] = offsets_ref[0:1, part]
        out_ref[SITE_ROWS + j : SITE_ROWS + j + 1, :] = offsets_ref[1:2, part]
        out_ref[2 * SITE_ROWS + j : 2 * SITE_ROWS + j + 1, :] = cell_ref[0:1, part].astype(
            jnp.float32
        )
    start = tile_ref[0] * TILE
    root = start // SITE_DEV
    first = (start - root * SITE_DEV) // LANES
    mine = row * cols + col == root
    for q in range(3):
        rows = out_ref[pl.ds(q * SITE_ROWS + first, TILE_ROWS), :]
        there = RAW + q * TILE_ROWS
        out_ref[there : there + TILE_ROWS, :] = jnp.where(mine, rows, 0.0)
    grid_y = cols * CELL_Y
    lane = lax.broadcasted_iota(jnp.int32, (1, LANES), 1) - col * CELL_Y
    terms = []
    for f in range(FIELDS):
        for a in range(CELL_X):
            line = jnp.zeros((1, LANES), jnp.float32)
            for b in range(CELL_Y):
                line = jnp.where(
                    lane == (f * CELL_X + a) * grid_y + b, est_ref[f, a, b], line
                )
            terms.append(line)
    while len(terms) > 1:
        terms = [x + y for x, y in zip(terms[::2], terms[1::2])]
    count = out_ref.shape[0] - RAW - HEAD
    index = lax.broadcasted_iota(jnp.int32, (count, LANES), 0)
    out_ref[RAW + HEAD :, :] = jnp.where(
        index == row, jnp.broadcast_to(terms[0], (count, LANES)), 0.0
    )


def smooth_pieces(get_raw, block_row, table_ref, rows_mesh, grid_y, result):
    total_x = CELL_X * rows_mesh
    state = {"numer": [None] * FIELDS, "sum_x": None}

    def begin():
        off_x, off_y, cell = get_raw()
        cell_x = jnp.floor((cell + 0.5) / grid_y)
        cell_y = cell - cell_x * grid_y
        state.update(cell_x=cell_x, loc_x=cell_x + off_x, loc_y=cell_y + off_y)
        weight_y = []
        for b in range(grid_y):
            dist = state["loc_y"] - (b + 0.5)
            value = jnp.exp(-dist * dist / (2.0 * spread_cells * spread_cells))
            weight_y.append(jnp.where(jnp.abs(cell_y - b) <= RADIUS, value, 0.0))
        state.update(weight_y=weight_y, sum_y=functools.reduce(jnp.add, weight_y))

    def add_column(a):
        coord = (block_row - 1) * CELL_X + a
        near = block_row - 1 + a // CELL_X
        line = HEAD + jnp.clip(near, 0, rows_mesh - 1)
        coord_f = coord.astype(jnp.float32)
        dist = state["loc_x"] - coord_f - 0.5
        value = jnp.exp(-dist * dist / (2.0 * spread_cells * spread_cells))
        inside = (coord >= 0) & (coord < total_x)
        reach = jnp.where(inside, float(RADIUS), -1.0)
        weight = jnp.where(jnp.abs(state["cell_x"] - coord_f) <= reach, value, 0.0)
        state["sum_x"] = weight if state["sum_x"] is None else state["sum_x"] + weight
        for f in range(FIELDS):
            base = (f * CELL_X + a % CELL_X) * grid_y
            inner = None
            for b in range(grid_y):
                term = table_ref[line, base + b] * state["weight_y"][b]
                inner = term if inner is None else inner + term
            term = inner * weight
            numer = state["numer"]
            numer[f] = term if numer[f] is None else numer[f] + term

    def end():
        denom = state["sum_x"] * state["sum_y"]
        result["fields"] = [n / denom for n in state["numer"]]
        result["loc"] = (state["loc_x"], state["loc_y"])

    columns = range(CELL_X - RADIUS, 2 * CELL_X + RADIUS)
    return (
        [(100, begin)]
        + [(150, functools.partial(add_column, a)) for a in columns]
        + [(20, end)]
    )


def smooth(raw, *args):
    result = {}
    for _, piece in smooth_pieces(lambda: raw, *args, result):
        piece()
    return result["fields"], *result["loc"]


def quantities(fields, loc_x, loc_y, centre, total_x):
    first = jnp.exp(2.0 * (fields[0] + range_shift))
    second = jnp.exp(2.0 * (fields[1] + range_shift))
    cosine = jnp.cos(fields[2])
    sine = jnp.sin(fields[2])
    m_a = (cosine * cosine * first + sine * sine * second) * (1.0 / 6.0)
    m_b = (sine * sine * first + cosine * cosine * second) * (1.0 / 6.0)
    m_c = (cosine * sine * (first - second)) * (1.0 / 6.0)
    return m_a, m_b, m_c, (loc_x - centre[0]) / total_x, (loc_y - centre[1]) / total_x


def log_root(fields):
    return fields[0] + fields[1] + 2.0 * range_shift


def site_scale(fields):
    return jnp.exp(fields[3] + 0.5 * log_root(fields)) * (3.0**-0.5)


def scaled_nugget(fields):
    return (3.0 * nugget_share) * jnp.exp(-log_root(fields))


def rows_of(quant):
    a, b, c, x, y = quant
    one = jnp.ones_like(a)
    own = b * x * x + a * y * y - 2.0 * c * x * y
    return [
        one,
        own,
        b,
        a,
        c,
        x * x,
        y * y,
        x * y,
        2.0 * (c * y - b * x),
        2.0 * (c * x - a * y),
        x,
        y,
        a * b - c * c,
    ]


def form_of(quant, weight):
    a, b, c, x, y = quant
    own = b * x * x + a * y * y - 2.0 * c * x * y
    values = [
        own,
        None,
        x * x,
        y * y,
        -2.0 * x * y,
        b,
        a,
        -2.0 * c,
        x,
        y,
        2.0 * (c * y - b * x),
        2.0 * (c * x - a * y),
    ]
    return [weight if v is None else v * weight for v in values]


def det_of(quant, weight):
    a, b, c, _, _ = quant
    values = [a * b - c * c, None, b, a, -2.0 * c]
    values = [v if v is None else v * weight for v in values]
    return {0: values[0], 2: values[3], 3: values[2], 4: values[4], 12: weight}


def thirds(values):
    high = values.astype(jnp.bfloat16)
    rest = values - high.astype(jnp.float32)
    low = rest.astype(jnp.bfloat16)
    return high, low, (rest - low.astype(jnp.float32)).astype(jnp.bfloat16)


LEFT_ORDER = (0, 0, 1, 1, 0, 2, 1, 2)
RIGHT_ORDER = (0, 1, 0, 1, 2, 0, 2, 1)


def covariance(det, form):
    inv_root = lax.rsqrt(det)
    form = jnp.maximum(form, 1e-36)
    dist = form * lax.rsqrt(form) * inv_root
    return (inv_root + inv_root * dist) * jnp.exp(-dist)


def halves(values):
    high = values.astype(jnp.bfloat16)
    return high, (values - high.astype(jnp.float32)).astype(jnp.bfloat16)


def left_parts(values):
    high, low = halves(values)
    return jnp.concatenate([high, high, low], axis=1)


def right_parts(values):
    high, low = halves(values)
    return jnp.concatenate([high, low, high], axis=0)


def dot_parts(left, right):
    return jnp.dot(left, right, preferred_element_type=jnp.float32)


def lane_copy(values, lane):
    index = jnp.full(values.shape, lane, jnp.int32)
    return jnp.take_along_axis(values, index, axis=1)


def row_copy(values, row):
    return jnp.broadcast_to(values[row : row + 1, :], values.shape)


def factor_step(m, work, lines_ref, own_ref):
    steps = BLOCK // 8
    lane = lax.broadcasted_iota(jnp.int32, (8, BLOCK), 1)
    sub = lax.broadcasted_iota(jnp.int32, (8, BLOCK), 0)
    at = 8 * m
    before = at - 8

    def row(i):
        return work[8 * i : 8 * i + 8, :]

    def set_row(i, values):
        work[8 * i : 8 * i + 8, :] = values

    def updated(values, first, lines):
        term = [lane_copy(values, first + c) * lines[c] for c in range(8)]
        total = ((term[0] + term[1]) + (term[2] + term[3])) + (
            (term[4] + term[5]) + (term[6] + term[7])
        )
        return jnp.where((lane >= first) & (lane < first + 8), 0.0, values) - total

    here = row(m)
    column = [lane_copy(here, at + c) for c in range(8)]
    if m > 0:
        if m + 1 < steps:
            past = [jnp.broadcast_to(lines_ref[c : c + 1, :], (8, BLOCK)) for c in range(8)]
            following = updated(row(m + 1), before, past)
        near = min(m + 2 + LANE_ROWS, steps)
        total = {}
        for c in range(8):
            for i in range(m + 2, near):
                term = lane_copy(row(i), before + c) * past[c]
                total[i] = term if c == 0 else total[i] + term
        for i in range(m + 2, near):
            gone = (lane >= before) & (lane < at)
            set_row(i, jnp.where(gone, 0.0, row(i)) - total[i])
        if near < steps:
            rest = work[8 * near :, :]
            gone = lax.broadcasted_iota(jnp.int32, rest.shape, 1)
            gone = (gone >= before) & (gone < at)
            work[8 * near :, :] = jnp.where(gone, 0.0, rest) - dot(
                rest[:, before:at], lines_ref[...]
            )
    elif m + 1 < steps:
        following = row(m + 1)
    pivots = (lane >= at) & (lane < at + 8)
    block = jnp.where(lane - at == sub, 1.0, jnp.where(pivots, 0.0, here))
    solved = jnp.zeros((8, BLOCK), jnp.float32)
    pairs = []
    for c in range(0, 8, 2):
        p = row_copy(column[c], c)
        r = row_copy(column[c + 1], c)
        q = row_copy(column[c + 1], c + 1)
        det = p * q - r * r
        inv = 1.0 / det
        both = (sub == c) | (sub == c + 1)
        first = jnp.where(both, 0.0, column[c])
        second = jnp.where(both, 0.0, column[c + 1])
        left = q * first - r * second
        right = p * second - r * first
        upper = row_copy(block, c)
        under = row_copy(block, c + 1)
        solved = jnp.where(sub == c, upper * lax.rsqrt(p), solved)
        solved = jnp.where(sub == c + 1, (p * under - r * upper) * lax.rsqrt(p * det), solved)
        pairs.append((p, r, q, inv))
        if c + 2 < 8:
            left_inv = left * inv
            right_inv = right * inv
            for j in range(c + 2, 8):
                a = row_copy(column[j], c)
                b = row_copy(column[j], c + 1)
                if j < c + 4:
                    column[j] = column[j] - (left * a + right * b) * inv
                else:
                    column[j] = (column[j] - left_inv * a) - right_inv * b
            block = (block - left_inv * upper) - right_inv * under
        else:
            block = block - (left * upper + right * under) * inv
    own_ref[at : at + 8, :] = jnp.where(lane <= at + sub, solved, 0.0)
    if m == steps - 1:
        return
    lines = []
    for h, (p, r, q, inv) in enumerate(pairs):
        upper = row_copy(block, 2 * h)
        under = row_copy(block, 2 * h + 1)
        lines.append((q * upper - r * under) * inv)
        lines.append((p * under - r * upper) * inv)
    set_row(m + 1, updated(following, at, lines))
    for c in range(8):
        lines_ref[c : c + 1, :] = lines[c][c : c + 1, :]


def at(block):
    return slice(block * BLOCK, (block + 1) * BLOCK)


def main_kernel(rows_mesh, cols, tile_ref, table_ref, buf_ref, *refs):
    packs = refs[:cols]
    (
        panel_ref,
        fields_ref,
        raws,
        nugget,
        scales,
        feats,
        panel_left,
        panel_det,
        panel_form,
        site_feats,
        site_det,
        site_form,
        gram,
        owns,
        lower,
        left,
        right,
        operand,
        work,
        lines_ref,
        residual,
        solved,
        raw_sems,
        sems,
    ) = refs[cols:]
    row = lax.axis_index("row")
    col = lax.axis_index("col")
    grid_y = cols * CELL_Y
    total_x = float(CELL_X * rows_mesh)
    width = TILE // cols
    start = tile_ref[0] * TILE
    root_row = start // (SITE_DEV * cols)
    blocks = TILE // BLOCK
    sites = cols * SITE_DEV
    chunks = sites // CHUNK
    site_lines = sites // LANES
    steps = BLOCK // 8
    lane = lax.broadcasted_iota(jnp.int32, (8, BLOCK), 1)
    sub = lax.broadcasted_iota(jnp.int32, (8, BLOCK), 0)
    centre = (
        (root_row * CELL_X).astype(jnp.float32) + 0.5 * CELL_X,
        0.5 * grid_y,
    )

    def raw_copy(k):
        return pltpu.make_async_copy(packs[k].at[0:RAW], raws.at[k], raw_sems.at[k])

    for k in range(cols):
        raw_copy(k).start()

    raw = [buf_ref[q * TILE_ROWS : (q + 1) * TILE_ROWS, :] for q in range(3)]
    fields, loc_x, loc_y = smooth(raw, root_row, table_ref, rows_mesh, grid_y)
    quant = quantities(fields, loc_x, loc_y, centre, total_x)
    nugget[...] = scaled_nugget(fields)
    one = jnp.ones_like(quant[0])
    feats[...] = jnp.zeros(feats.shape, jnp.float32)
    for n, values in enumerate((rows_of(quant), form_of(quant, one), det_of(quant, one))):
        values = values if isinstance(values, dict) else dict(enumerate(values))
        for f, value in values.items():
            for g in range(TILE_ROWS):
                feats[n, f : f + 1, g * LANES : (g + 1) * LANES] = value[g : g + 1, :]
    for k in range(cols):
        raw_copy(k).wait()

    def put_parts(target, values, lanes):
        parts = thirds(values)
        for n, part in enumerate(RIGHT_ORDER):
            target[n * FEATURES : (n + 1) * FEATURES, lanes] = parts[part]

    def panel_features(g):
        lanes = slice(g * LANES, (g + 1) * LANES)
        parts = [p.astype(jnp.float32) for p in thirds(feats[0, :, lanes])]
        stack = jnp.concatenate([parts[part] for part in LEFT_ORDER], axis=0)
        panel_left[lanes, :] = jnp.transpose(stack).astype(jnp.bfloat16)
        put_parts(panel_form, feats[1, :, lanes], lanes)
        put_parts(panel_det, feats[2, :, lanes], lanes)

    def panel_gram(i, j):
        gram[at(i), at(j)] = covariance(
            dot_parts(panel_left[at(i), :], panel_det[:, at(j)]),
            dot_parts(panel_left[at(i), :], panel_form[:, at(j)]),
        )

    def site_rows():
        raw = [
            jnp.concatenate(
                [raws[k, q * SITE_ROWS : (q + 1) * SITE_ROWS, :] for k in range(cols)], axis=0
            )
            for q in range(3)
        ]
        fields, loc_x, loc_y = smooth(raw, row, table_ref, rows_mesh, grid_y)
        for f in range(FIELDS):
            for j in range(SITE_ROWS):
                fields_ref[f : f + 1, j * LANES : (j + 1) * LANES] = fields[f][j : j + 1, :]
        quant = quantities(fields, loc_x, loc_y, centre, total_x)
        scale = site_scale(fields)
        inverse = 1.0 / scale
        weight = inverse * inverse
        site_feats[...] = jnp.zeros(site_feats.shape, jnp.float32)
        for k in range(cols):
            member = jnp.bitwise_xor(col, k) * SITE_ROWS
            mine = slice(k * SITE_ROWS, (k + 1) * SITE_ROWS)
            scales[pl.ds(pl.multiple_of(member, 8), SITE_ROWS), :] = scale[mine, :]
            for n, values in enumerate((form_of(quant, weight), det_of(quant, weight))):
                values = values if isinstance(values, dict) else dict(enumerate(values))
                for f, value in values.items():
                    for j in range(SITE_ROWS):
                        there = pl.multiple_of((member + j) * LANES, LANES)
                        at_row = k * SITE_ROWS + j
                        site_feats[n, f : f + 1, pl.ds(there, LANES)] = value[
                            at_row : at_row + 1, :
                        ]

    def site_parts(line):
        lanes = slice(line * LANES, (line + 1) * LANES)
        put_parts(site_form, site_feats[0, :, lanes], lanes)
        put_parts(site_det, site_feats[1, :, lanes], lanes)

    def copy_out(b, part):
        there = slice(b * BLOCK % width, b * BLOCK % width + BLOCK)
        return pltpu.make_async_copy(
            solved.at[at(b), part], panel_ref.at[there, part], sems.at[b]
        )

    def wide(j):
        return slice(3 * j * BLOCK, 3 * (j + 1) * BLOCK)

    def chunk_of(ch):
        return slice(ch * CHUNK, (ch + 1) * CHUNK)

    taken = set()
    fresh = set()

    def fresh_line(k, line):
        lanes = slice(line * LANES, (line + 1) * LANES)
        value = covariance(
            dot_parts(panel_left[at(k), :], site_det[:, lanes]),
            dot_parts(panel_left[at(k), :], site_form[:, lanes]),
        )
        fresh.add((k, line))
        if (k, line) in taken:
            value = value + residual[k % 2, :, lanes]
        residual[k % 2, :, lanes] = value

    def take_solved(k, ch):
        values = dot_parts(left[at(k), : 3 * k * BLOCK], right[: 3 * k * BLOCK, chunk_of(ch)])
        for p in range(CHUNK // LANES):
            line = ch * (CHUNK // LANES) + p
            lanes = slice(line * LANES, (line + 1) * LANES)
            part = values[:, p * LANES : (p + 1) * LANES]
            taken.add((k, line))
            residual[k % 2, :, lanes] = (
                residual[k % 2, :, lanes] - part if (k, line) in fresh else -part
            )

    def split_residual(k, ch):
        operand[ch % 2] = right_parts(residual[k % 2, :, chunk_of(ch)])

    def solve_chunk(k, ch):
        solved[at(k), chunk_of(ch)] = dot_parts(left[at(k), wide(k)], operand[ch % 2])

    def split_solved(k, ch):
        right[wide(k), chunk_of(ch)] = right_parts(solved[at(k), chunk_of(ch)])

    def lower_block(i, k):
        values = dot_t(gram[at(i), at(k)], owns[k])
        lower[at(i), at(k)] = values
        left[at(i), wide(k)] = left_parts(values)

    def update_block(i, j, k):
        gram[at(i), at(j)] = gram[at(i), at(j)] - dot_t(lower[at(i), at(k)], lower[at(j), at(k)])

    def stretch(code):
        pl.when(tile_ref[0] >= 0)(code)

    def shared(count, m):
        return [n for n in range(count) if n * steps // count == m]

    def beside(k, m):
        if k == 0:
            pairs = [(i, j) for i in range(1, blocks) for j in range(i + 1)]
            if m == 0:
                for g in range(1, TILE_ROWS):
                    panel_features(g)
            for n in shared(len(pairs), m - 1) if m > 0 else ():
                panel_gram(*pairs[n])
            for line in shared(site_lines, m):
                site_parts(line)
            for line in shared(site_lines, m - 1) if m > 0 else ():
                fresh_line(0, line)
            return
        others = [(i, j) for i in range(k + 1, blocks) for j in range(k, i + 1)]
        if 0 < m <= len(others):
            update_block(*others[m - 1], k - 1)
        for line in shared(site_lines, m):
            fresh_line(k, line)
        period = steps // chunks
        ch = m // period
        if m % period == 0:
            if m == 0:
                split_residual(k - 1, 0)
            solve_chunk(k - 1, ch)
        if m % period == period - 1:
            if ch + 1 < chunks:
                split_residual(k - 1, ch + 1)
            split_solved(k - 1, ch)
            if ch > 0:
                take_solved(k, ch - 1)

    def beside_update(k):
        if k == 0:
            for line in shared(site_lines, steps - 1):
                fresh_line(0, line)
            return
        take_solved(k, chunks - 1)

    site_rows()
    panel_features(0)
    panel_gram(0, 0)
    for k in range(blocks):

        for first in range(0, steps, STRETCH):

            @stretch
            def _(k=k, first=first):
                for i in range(steps) if first == 0 else ():
                    rows = slice(8 * i, 8 * i + 8)
                    values = gram[k * BLOCK + 8 * i : k * BLOCK + 8 * i + 8, at(k)]
                    nug = jnp.broadcast_to(nugget[k : k + 1, :], (8, BLOCK))
                    work[rows, :] = values + jnp.where(lane - 8 * i == sub, nug, 0.0)
                for m in range(first, first + STRETCH):
                    factor_step(m, work, lines_ref, owns.at[k])
                    beside(k, m)

        @stretch
        def _(k=k):
            if k + 1 < blocks:
                lower_block(k + 1, k)
                update_block(k + 1, k + 1, k)
            for i in range(k + 2, blocks):
                lower_block(i, k)
            left[at(k), wide(k)] = left_parts(owns[k])
            beside_update(k)

        if k > 0:

            @pl.when(col == (k - 1) * BLOCK // width)
            def _(k=k):
                copy_out(k - 1, slice(None)).start()

        offset = start + k * BLOCK - row * sites

        @pl.when((offset >= 0) & (offset < sites))
        def _(k=k, offset=offset):
            nug = nugget[k : k + 1, :] * scales[pl.ds(offset // LANES, 1), :]
            here = pl.ds(pl.multiple_of(offset, LANES), LANES)
            for i in range(steps):
                rows = slice(8 * i, 8 * i + 8)
                residual[k % 2, rows, here] = residual[k % 2, rows, here] + jnp.where(
                    lane - 8 * i == sub, jnp.broadcast_to(nug, (8, LANES)), 0.0
                )

    last = blocks - 1
    mine = col == last * BLOCK // width
    for ch in range(chunks):
        part = slice(ch * CHUNK, (ch + 1) * CHUNK)
        split_residual(last, ch)
        solve_chunk(last, ch)

        @pl.when(mine)
        def _(part=part):
            copy_out(last, part).start()

    for b in range(blocks):

        @pl.when(col == b * BLOCK // width)
        def _(b=b):
            copy_out(b, slice(None)).wait()


def body(offsets, site_cell, estimates, panel_tile):
    rows_mesh = lax.axis_size("row")
    cols = lax.axis_size("col")
    devices = rows_mesh * cols
    assert FIELDS * CELL_X * CELL_Y * cols == LANES
    assert devices & (devices - 1) == 0
    vmem = pl.BlockSpec(memory_space=pltpu.VMEM)
    smem = pl.BlockSpec(memory_space=pltpu.SMEM)
    pack = pl.pallas_call(
        functools.partial(pack_kernel, cols),
        out_shape=jax.ShapeDtypeStruct((RAW + HEAD + rows_mesh, LANES), jnp.float32),
        in_specs=[smem, smem, vmem, vmem],
        out_specs=vmem,
    )(panel_tile, estimates, offsets, site_cell.reshape(1, -1))
    packs = [pack]
    buf = pack[RAW:]
    step = 1
    while step < devices:
        pairs = [(i, i ^ step) for i in range(devices)]
        if step < cols:
            sent = jnp.concatenate([pack[:RAW], buf], axis=0) if step > 1 else pack
            near = lax.ppermute(sent, ("row", "col"), pairs)
            packs.append(near)
            for k in range(1, step):
                far = lax.ppermute(packs[k], ("row", "col"), pairs)
                packs.append(far)
            buf = buf + near[RAW:]
        else:
            buf = buf + lax.ppermute(buf, ("row", "col"), pairs)
        step *= 2
    width = TILE // cols
    sites = cols * SITE_DEV
    anywhere = pl.BlockSpec(memory_space=pl.ANY)
    panel, fields = pl.pallas_call(
        functools.partial(main_kernel, rows_mesh, cols),
        out_shape=(
            jax.ShapeDtypeStruct((width, sites), jnp.float32),
            jax.ShapeDtypeStruct((FIELDS, SITE_DEV), jnp.float32),
        ),
        in_specs=[smem, smem, vmem] + [anywhere] * cols,
        out_specs=(anywhere, vmem),
        scratch_shapes=[
            pltpu.VMEM((cols, RAW, LANES), jnp.float32),
            pltpu.VMEM((TILE_ROWS, LANES), jnp.float32),
            pltpu.VMEM((cols * SITE_ROWS, LANES), jnp.float32),
            pltpu.VMEM((3, FEATURES, TILE), jnp.float32),
            pltpu.VMEM((TILE, COPIES * FEATURES), jnp.bfloat16),
            pltpu.VMEM((COPIES * FEATURES, TILE), jnp.bfloat16),
            pltpu.VMEM((COPIES * FEATURES, TILE), jnp.bfloat16),
            pltpu.VMEM((2, FEATURES, sites), jnp.float32),
            pltpu.VMEM((COPIES * FEATURES, sites), jnp.bfloat16),
            pltpu.VMEM((COPIES * FEATURES, sites), jnp.bfloat16),
            pltpu.VMEM((TILE, TILE), jnp.float32),
            pltpu.VMEM((TILE // BLOCK, BLOCK, BLOCK), jnp.float32),
            pltpu.VMEM((TILE, TILE), jnp.float32),
            pltpu.VMEM((TILE, 3 * TILE), jnp.bfloat16),
            pltpu.VMEM((3 * (TILE - BLOCK), sites), jnp.bfloat16),
            pltpu.VMEM((2, 3 * BLOCK, CHUNK), jnp.bfloat16),
            pltpu.VMEM((BLOCK, BLOCK), jnp.float32),
            pltpu.VMEM((8, BLOCK), jnp.float32),
            pltpu.VMEM((2, BLOCK, sites), jnp.float32),
            pltpu.VMEM((TILE, sites), jnp.float32),
            pltpu.SemaphoreType.DMA((cols,)),
            pltpu.SemaphoreType.DMA((TILE // BLOCK,)),
        ],
        compiler_params=pltpu.CompilerParams(vmem_limit_bytes=40 * 1024 * 1024),
    )(panel_tile, buf, buf, *packs)
    return (panel, fields)


def solution(mesh):
    placed = (P(None, ("row", "col")), P(("row", "col")), P(None, "row", "col"), P())
    return jax.shard_map(
        body,
        mesh=mesh,
        in_specs=placed,
        out_specs=(P("col", "row"), P(None, ("row", "col"))),
        check_vma=False,
    )
```

time: 46.3 us -> 42 us (0.907)
  Pallas kernels: 24.6 us -> 20.3 us
    pallas_call x1, Pallas kernels: 23.2 us -> 18.8 us  [body(): pl.pallas_call(functools.partial(main_kernel, rows_mesh, cols), out_shape...]
where the time goes in v3:
time: 42 us; the launch traced here: 41.6 us
  Pallas kernels  20.3 us (48%)
  starting transfers between devices  10.5 us (25%)
  waiting for transfers between devices  7.93 us (19%)
  between operations  1.45 us (3%)
  local copies, waits for them, and re-layouts  0.75 us (2%)
  other arithmetic  0.74 us (2%)
    pallas_call x1, Pallas kernels, body(): pl.pallas_call(functools.partial(main_kernel, rows_mesh, cols), out_shape...  18.8 us
    ppermute x4, starting transfers between devices, body(): buf = buf + lax.ppermute(buf, ('row', 'col'), pairs)  9.99 us
    ppermute x4, waiting for transfers between devices, body(): buf = buf + lax.ppermute(buf, ('row', 'col'), pairs)  6.86 us
    pallas_call x1, Pallas kernels, body(): pl.pallas_call(functools.partial(pack_kernel, cols), out_shape=jax.ShapeD...  1.46 us
    ppermute x1, waiting for transfers between devices, body(): near = lax.ppermute(sent, ('row', 'col'), pairs)  1.07 us
  transfers between devices with their start and end apart: 5, of which 5 were waited for; matrix products, arithmetic and copies ran while one was open for 0% of the time, Pallas kernels for 0%

profile of v3, /device:TPU:0, one launch (start us, length us, event | category | flops | bytes accessed | tf_op | source)
XLA Modules:
  0.0 41.6 jit_solution(17185202851946056066)
XLA Ops:
  1.3 1.5 %shard_map.59.refs_0_ = f32[52,128]{1,0:T(8,128)} custom-call(s32[1]{0:T(128)S(6)} %copy.6.tile_ref, f32[4,4,4]{2,1,0:T(4,128)} %est_ref.1, f32[2,1024]{1,0:T(2,128)} %offsets_ref.1, s32[1,1024]{1,0:T(1,128)} %bitcast.1), custom_call_target="tpu_custom_call" | custom-call | tf_op jit(solution)/shard_map/pallas_call | solution.py:644
  2.7 0.5 %collective-permute-start = (f32[52,128]{1,0:T(8,128)}, f32[52,128]{1,0:T(8,128)S(1)}, u32[]{:S(2)}, u32[]{:S(2)}) collective-permute-start(f32[52,128]{1,0:T(8,128)} %shard_map.59.refs_0_), channel_id=1, source_target_pairs={{0,1},{1,0},{2,3},{3,2},{4,5},{5,4},{6,7},{7,6},{8,9},{9,8},{10,11... | collective-permute-start | bytes 79880 | tf_op jit(solution)/shard_map/ppermute | solution.py:657
  3.2 1.1 %collective-permute-done.refs_1_ = f32[52,128]{1,0:T(8,128)S(1)} collective-permute-done((f32[52,128]{1,0:T(8,128)}, f32[52,128]{1,0:T(8,128)S(1)}, u32[]{:S(2)}, u32[]{:S(2)}) %collective-permute-start) | collective-permute-done | bytes 26656 | tf_op jit(solution)/shard_map/ppermute | solution.py:657
  4.3 0.7 %slice_add_fusion = f32[28,128]{1,0:T(8,128)S(1)} fusion(f32[52,128]{1,0:T(8,128)S(1)} %collective-permute-done.refs_1_, f32[52,128]{1,0:T(8,128)} %shard_map.59.refs_0_), kind=kLoop, calls=%fused_computation | loop fusion | flops 3584 | bytes 43008 | tf_op jit(solution)/shard_map/add | solution.py:662
  5.0 2.8 %collective-permute-start.1 = (f32[28,128]{1,0:T(8,128)S(1)}, f32[28,128]{1,0:T(8,128)S(1)}, u32[]{:S(2)}, u32[]{:S(2)}) collective-permute-start(f32[28,128]{1,0:T(8,128)S(1)} %slice_add_fusion), channel_id=1, source_target_pairs={{0,2},{1,3},{2,0},{3,1},{4,6},{5,7},{6,4},{7,5},{8,10},{9,11},{10,... | collective-permute-start | bytes 43016 | tf_op jit(solution)/shard_map/ppermute | solution.py:664
  7.8 1.7 %collective-permute-done.1 = f32[28,128]{1,0:T(8,128)S(1)} collective-permute-done((f32[28,128]{1,0:T(8,128)S(1)}, f32[28,128]{1,0:T(8,128)S(1)}, u32[]{:S(2)}, u32[]{:S(2)}) %collective-permute-start.1) | collective-permute-done | bytes 14368 | tf_op jit(solution)/shard_map/ppermute | solution.py:664
  9.6 2.1 %collective-permute-start.2 = (f32[28,128]{1,0:T(8,128)S(1)}, f32[28,128]{1,0:T(8,128)S(1)}, u32[]{:S(2)}, u32[]{:S(2)}) collective-permute-start(f32[28,128]{1,0:T(8,128)S(1)} %add.16), channel_id=1, source_target_pairs={{0,4},{1,5},{2,6},{3,7},{4,0},{5,1},{6,2},{7,3},{8,12},{9,13},{10,... | collective-permute-start | bytes 43016 | tf_op jit(solution)/shard_map/ppermute | solution.py:664
  11.6 1.7 %collective-permute-done.2 = f32[28,128]{1,0:T(8,128)S(1)} collective-permute-done((f32[28,128]{1,0:T(8,128)S(1)}, f32[28,128]{1,0:T(8,128)S(1)}, u32[]{:S(2)}, u32[]{:S(2)}) %collective-permute-start.2) | collective-permute-done | bytes 14368 | tf_op jit(solution)/shard_map/ppermute | solution.py:664
  13.3 2.1 %collective-permute-start.3 = (f32[28,128]{1,0:T(8,128)S(1)}, f32[28,128]{1,0:T(8,128)S(1)}, u32[]{:S(2)}, u32[]{:S(2)}) collective-permute-start(f32[28,128]{1,0:T(8,128)S(1)} %add.17), channel_id=1, source_target_pairs={{0,8},{1,9},{2,10},{3,11},{4,12},{5,13},{6,14},{7,15},{8,0},{9,1},... | collective-permute-start | bytes 43016 | tf_op jit(solution)/shard_map/ppermute | solution.py:664
  15.4 1.7 %collective-permute-done.3 = f32[28,128]{1,0:T(8,128)S(1)} collective-permute-done((f32[28,128]{1,0:T(8,128)S(1)}, f32[28,128]{1,0:T(8,128)S(1)}, u32[]{:S(2)}, u32[]{:S(2)}) %collective-permute-start.3) | collective-permute-done | bytes 14368 | tf_op jit(solution)/shard_map/ppermute | solution.py:664
  17.1 3.0 %collective-permute-start.4 = (f32[28,128]{1,0:T(8,128)S(1)}, f32[28,128]{1,0:T(8,128)S(1)}, u32[]{:S(2)}, u32[]{:S(2)}) collective-permute-start(f32[28,128]{1,0:T(8,128)S(1)} %add.18), channel_id=1, source_target_pairs={{0,16},{1,17},{2,18},{3,19},{4,20},{5,21},{6,22},{7,23},{8,24},{9,... | collective-permute-start | bytes 43016 | tf_op jit(solution)/shard_map/ppermute | solution.py:664
  20.2 1.7 %collective-permute-done.4 = f32[28,128]{1,0:T(8,128)S(1)} collective-permute-done((f32[28,128]{1,0:T(8,128)S(1)}, f32[28,128]{1,0:T(8,128)S(1)}, u32[]{:S(2)}, u32[]{:S(2)}) %collective-permute-start.4) | collective-permute-done | bytes 14368 | tf_op jit(solution)/shard_map/ppermute | solution.py:664
  21.9 0.0 copy-start
  21.9 0.7 %copy-done = f32[52,128]{1,0:T(8,128)S(1)} copy-done((f32[52,128]{1,0:T(8,128)S(1)}, f32[52,128]{1,0:T(8,128)}, u32[]{:S(2)}) %copy-start) | copy-done | bytes 26648
  22.6 18.8 %shard_map.60 = (f32[256,2048]{1,0:T(8,128)}, f32[4,1024]{1,0:T(4,128)}) custom-call(s32[1]{0:T(128)S(6)} %copy.6.tile_ref, f32[28,128]{1,0:T(8,128)S(1)} %add.19.table_ref.buf_ref, f32[28,128]{1,0:T(8,128)S(1)} %add.19.table_ref.buf_ref, f32[52,128]{1,0:T(8,128)S(1)} %copy-done, f32[52,128]{1,0:T(8,128)S(1)} %collective-permute-done.refs_1_), custom_call_target="tpu_custom_call" | custom-call | tf_op jit(solution)/shard_map/pallas_call | solution.py:669
  (4 shorter events, 0.0 us)
Async XLA Ops:
  2.7 1.6 %collective-permute-start = (f32[52,128]{1,0:T(8,128)}, f32[52,128]{1,0:T(8,128)S(1)}, u32[]{:S(2)}, u32[]{:S(2)}) collective-permute-start(f32[52,128]{1,0:T(8,128)} %shard_map.59.refs_0_), channel_id=1, source_target_pairs={{0,1},{1,0},{2,3},{3,2},{4,5},{5,4},{6,7},{7,6},{8,9},{9,8},{10,11... | collective-permute-start | bytes 79880 | tf_op jit(solution)/shard_map/ppermute | solution.py:657
  5.0 4.5 %collective-permute-start.1 = (f32[28,128]{1,0:T(8,128)S(1)}, f32[28,128]{1,0:T(8,128)S(1)}, u32[]{:S(2)}, u32[]{:S(2)}) collective-permute-start(f32[28,128]{1,0:T(8,128)S(1)} %slice_add_fusion), channel_id=1, source_target_pairs={{0,2},{1,3},{2,0},{3,1},{4,6},{5,7},{6,4},{7,5},{8,10},{9,11},{10,... | collective-permute-start | bytes 43016 | tf_op jit(solution)/shard_map/ppermute | solution.py:664
  9.6 3.8 %collective-permute-start.2 = (f32[28,128]{1,0:T(8,128)S(1)}, f32[28,128]{1,0:T(8,128)S(1)}, u32[]{:S(2)}, u32[]{:S(2)}) collective-permute-start(f32[28,128]{1,0:T(8,128)S(1)} %add.16), channel_id=1, source_target_pairs={{0,4},{1,5},{2,6},{3,7},{4,0},{5,1},{6,2},{7,3},{8,12},{9,13},{10,... | collective-permute-start | bytes 43016 | tf_op jit(solution)/shard_map/ppermute | solution.py:664
  13.3 3.8 %collective-permute-start.3 = (f32[28,128]{1,0:T(8,128)S(1)}, f32[28,128]{1,0:T(8,128)S(1)}, u32[]{:S(2)}, u32[]{:S(2)}) collective-permute-start(f32[28,128]{1,0:T(8,128)S(1)} %add.17), channel_id=1, source_target_pairs={{0,8},{1,9},{2,10},{3,11},{4,12},{5,13},{6,14},{7,15},{8,0},{9,1},... | collective-permute-start | bytes 43016 | tf_op jit(solution)/shard_map/ppermute | solution.py:664
  17.1 4.8 %collective-permute-start.4 = (f32[28,128]{1,0:T(8,128)S(1)}, f32[28,128]{1,0:T(8,128)S(1)}, u32[]{:S(2)}, u32[]{:S(2)}) collective-permute-start(f32[28,128]{1,0:T(8,128)S(1)} %add.18), channel_id=1, source_target_pairs={{0,16},{1,17},{2,18},{3,19},{4,20},{5,21},{6,22},{7,23},{8,24},{9,... | collective-permute-start | bytes 43016 | tf_op jit(solution)/shard_map/ppermute | solution.py:664
  21.9 0.7 %copy-start = (f32[52,128]{1,0:T(8,128)S(1)}, f32[52,128]{1,0:T(8,128)}, u32[]{:S(2)}) copy-start(f32[52,128]{1,0:T(8,128)} %shard_map.59.refs_0_) | copy-start | bytes 79876
